TPU v7x, 768 devices: a whole 4x8x12 slice. The times are simulated.
768 devices in a mesh: ctx: 64 (over x, y, core), head: 12 (over z).
Axes of the slice: x: 4, y: 8, z: 12, core: 2. Of those that a mesh axis runs over, the one named last changes fastest.
Arguments:
- prompt_q: bfloat16 [8192, 36, 128], P('ctx', 'head'), may hold values from -6 to 6
- prompt_k: bfloat16 [8192, 36, 128], P('ctx', 'head'), may hold values from -6 to 6
- prompt_v: bfloat16 [8192, 36, 128], P('ctx', 'head'), may hold values from -6 to 6
- resp_q: bfloat16 [2, 4096, 36, 128], P(None, 'ctx', 'head'), may hold values from -6 to 6
- resp_k: bfloat16 [2, 4096, 36, 128], P(None, 'ctx', 'head'), may hold values from -6 to 6
- resp_v: bfloat16 [2, 4096, 36, 128], P(None, 'ctx', 'head'), may hold values from -6 to 6
- decay_rate: float32 [36], P('head'), may hold values from 8.138021e-06 to 0.033
- norm_gain: float32 [36, 128], P('head'), may hold values from 0.1 to 1.9
- prompt_cot: bfloat16 [8192, 36, 128], P('ctx', 'head'), may hold values from -6 to 6
- resp_cot: bfloat16 [2, 4096, 36, 128], P(None, 'ctx', 'head'), may hold values from -6 to 6
Outputs:
- prompt_y: bfloat16 [8192, 36, 128], P('ctx', 'head')
- resp_y: bfloat16 [2, 4096, 36, 128], P(None, 'ctx', 'head')
- prompt_dq: bfloat16 [8192, 36, 128], P('ctx', 'head')
- prompt_dk: bfloat16 [8192, 36, 128], P('ctx', 'head')
- prompt_dv: bfloat16 [8192, 36, 128], P('ctx', 'head')
- resp_dq: bfloat16 [2, 4096, 36, 128], P(None, 'ctx', 'head')
- resp_dk: bfloat16 [2, 4096, 36, 128], P(None, 'ctx', 'head')
- resp_dv: bfloat16 [2, 4096, 36, 128], P(None, 'ctx', 'head')
All inputs are finite; a program needn't handle non-finite values.
Results may differ from a plain program's by a relative error of at most 0.0062.
Values sent between devices are 32-bit elements; how exact they have to be, the bound alone decides.
A program may use at most 128 MiB of HBM per device.

v0:
```python
import jax
import jax.numpy as jnp
from jax import lax
from jax.sharding import Mesh
from jax.sharding import PartitionSpec as P

BLK = 64
CTX = ("ctx_0", "ctx_1", "ctx_2")


F32 = jnp.float32
BF16 = jnp.bfloat16


def nothing_yet(x, identity):
    return jax.tree.map(
        lambda part, zero: jnp.zeros_like(part) + jnp.asarray(zero, part.dtype), x, identity
    )


def gathered_once(x, axis):
    leaves = jax.tree.leaves(x)
    order = sorted(range(len(leaves)), key=lambda k: -leaves[k].size)
    width = (1, *leaves[order[0]].shape)[-1]
    lines = [
        jnp.pad(leaves[k].reshape(-1), (0, -leaves[k].size % width)).reshape(-1, width)
        for k in order
    ]
    both, at, found = (lax.all_gather(jnp.concatenate(lines), axis), 0, {})
    for k, line in zip(order, lines):
        share = both[:, at : at + len(line)].reshape(len(both), -1)
        found[k] = share[:, : leaves[k].size].reshape(-1, *leaves[k].shape)
        at += len(line)
    numbers = iter(range(len(leaves)))
    return jax.tree.map(lambda _: found[next(numbers)], x)


def entering(x, axes, combine, identity, reverse):
    before = start = nothing_yet(x, identity)
    subtotal = x
    for axis in reversed(axes):
        devices, position = (lax.axis_size(axis), lax.axis_index(axis))
        pieces = gathered_once(subtotal, axis)
        inside, subtotal = (start, start)
        for k in reversed(range(devices)) if reverse else range(devices):
            passed = k > position if reverse else k < position
            subtotal = combine(subtotal, jax.tree.map(lambda part: part[k], pieces))
            inside = jax.tree.map(lambda new, old: jnp.where(passed, new, old), subtotal, inside)
        before = combine(inside, before)
    return before


def broadcast(x, axis, root):
    return lax.dynamic_index_in_dim(lax.all_gather(x, axis), root, 0, keepdims=False)


def from_everyone(x, axis):
    copies = jnp.broadcast_to(x, (lax.axis_size(axis), *x.shape))
    return lax.all_to_all(copies, axis, split_axis=0, concat_axis=0, tiled=True)


def over_copies(x, axis):
    return from_everyone(x, axis).sum(axis=0)


def together(arrays, axis):
    line, at, finished = (jnp.concatenate([a.reshape(-1) for a in arrays]), 0, [])
    subtotal = over_copies(line, axis)
    for a in arrays:
        finished.append(subtotal[at : at + a.size].reshape(a.shape))
        at += a.size
    return tuple(finished)


def contract(form, left, right):
    return jnp.einsum(form, left, right, preferred_element_type=F32)


def powers(rates, steps):
    return jnp.exp(-rates[:, None] * steps[None, :])


def decay_mask(rates, length):
    places = jnp.arange(length, dtype=F32)
    offset = places[:, None] - places[None, :]
    decays = jnp.exp(-rates[:, None, None] * jnp.maximum(offset, 0.0)[None])
    return jnp.where((offset >= 0.0)[None], decays, 0.0)


def key_term(keys, values, rates):
    length = keys.shape[0]
    places = jnp.arange(length, dtype=F32)
    factor = powers(rates, length - 1.0 - places).T[:, :, None]
    keys_decayed = (keys.astype(F32) * factor).astype(BF16)
    return contract("shd,she->hde", keys_decayed, values)


def query_term(queries, grad_out, rates):
    length = queries.shape[0]
    places = jnp.arange(length, dtype=F32)
    factor = powers(rates, places + 1.0).T[:, :, None]
    queries_decayed = (queries.astype(F32) * factor).astype(BF16)
    return contract("jhd,jhe->hde", queries_decayed, grad_out)


def block_forward(queries, keys, values, carried, rates):
    length = queries.shape[0]
    places = jnp.arange(length, dtype=F32)
    scores = contract("jhd,shd->hjs", queries, keys)
    mixing = (scores * decay_mask(rates, length)).astype(BF16)
    within = contract("hjs,shd->jhd", mixing, values)
    across = (
        contract("jhd,hde->jhe", queries, carried.astype(BF16))
        * powers(rates, places + 1.0).T[:, :, None]
    )
    following = jnp.exp(-rates * length)[:, None, None] * carried + key_term(keys, values, rates)
    return (within + across, following)


def block_backward(queries, keys, values, grad_out, carried, later_grad, rates):
    length = queries.shape[0]
    places = jnp.arange(length, dtype=F32)
    masking = decay_mask(rates, length)
    mixing = (contract("jhd,shd->hjs", queries, keys) * masking).astype(BF16)
    dmixing = (contract("jhe,she->hjs", grad_out, values) * masking).astype(BF16)
    query_decay = powers(rates, places + 1.0).T[:, :, None]
    key_decay = powers(rates, length - 1.0 - places).T[:, :, None]
    later_bf = later_grad.astype(BF16)
    grad_q = contract("hjs,shd->jhd", dmixing, keys) + query_decay * contract(
        "jhe,hde->jhd", grad_out, carried.astype(BF16)
    )
    grad_k = contract("hjs,jhd->shd", dmixing, queries) + key_decay * contract(
        "she,hde->shd", values, later_bf
    )
    grad_v = contract("hjs,jhe->she", mixing, grad_out) + key_decay * contract(
        "shd,hde->she", keys, later_bf
    )
    earlier = jnp.exp(-rates * length)[:, None, None] * later_grad + query_term(
        queries, grad_out, rates
    )
    return (grad_q, grad_k, grad_v, earlier)


def split_blocks(array, block):
    return array.reshape((array.shape[0] // block, block) + array.shape[1:])


def chain_forward(queries, keys, values, carried, rates, block):

    def chain_advance(state_now, pieces):
        outputs, following = block_forward(pieces[0], pieces[1], pieces[2], state_now, rates)
        return (following, (outputs, state_now))

    pieces = (split_blocks(queries, block), split_blocks(keys, block), split_blocks(values, block))
    final_state, (outputs, entries) = lax.scan(chain_advance, carried, pieces)
    return (outputs.reshape(queries.shape), entries, final_state)


def chain_backward(queries, keys, values, grad_out, entries, later_grad, rates, block):

    def chain_retreat(grad_now, pieces):
        grad_q, grad_k, grad_v, earlier = block_backward(
            pieces[0], pieces[1], pieces[2], pieces[3], pieces[4], grad_now, rates
        )
        return (earlier, (grad_q, grad_k, grad_v))

    pieces = (
        split_blocks(queries, block),
        split_blocks(keys, block),
        split_blocks(values, block),
        split_blocks(grad_out, block),
        entries,
    )
    start_grad, (grad_q, grad_k, grad_v) = lax.scan(chain_retreat, later_grad, pieces, reverse=True)
    return (
        grad_q.reshape(queries.shape),
        grad_k.reshape(queries.shape),
        grad_v.reshape(queries.shape),
        start_grad,
    )


def key_state(keys, values, rates, zero_state, block):

    def key_advance(state_now, pieces):
        return (
            jnp.exp(-rates * block)[:, None, None] * state_now
            + key_term(pieces[0], pieces[1], rates),
            None,
        )

    result, ignored = lax.scan(
        key_advance, zero_state, (split_blocks(keys, block), split_blocks(values, block))
    )
    return result


def query_state(queries, grad_out, rates, zero_state, block):

    def query_retreat(grad_now, pieces):
        return (
            jnp.exp(-rates * block)[:, None, None] * grad_now
            + query_term(pieces[0], pieces[1], rates),
            None,
        )

    result, ignored = lax.scan(
        query_retreat,
        zero_state,
        (split_blocks(queries, block), split_blocks(grad_out, block)),
        reverse=True,
    )
    return result


def combine_all(earlier, later):
    return (
        later[0] + later[1][:, None, None] * earlier[0],
        earlier[1] * later[1],
        later[2] + later[3][:, None, None] * earlier[2],
        earlier[3] * later[3],
    )


def norm_sums(outputs, cotangent, norm_gain):
    square_sum = jnp.sum(outputs * outputs, axis=(1, 2))
    inner_sum = jnp.sum(norm_gain[None] * cotangent.astype(F32) * outputs, axis=(1, 2))
    return (square_sum, inner_sum)


def norm_finish(outputs, cotangent, norm_gain, square_sum, inner_sum, features):
    inv_rms = lax.rsqrt(square_sum / features + 1e-05)[:, None, None]
    normed = (norm_gain[None] * outputs * inv_rms).astype(BF16)
    cubed = inv_rms * inv_rms * inv_rms
    grad = (
        norm_gain[None] * cotangent.astype(F32) * inv_rms
        - outputs * inner_sum[:, None, None] * cubed / features
    ).astype(BF16)
    return (normed, grad)


def shards(
    prompt_q,
    prompt_k,
    prompt_v,
    resp_q,
    resp_k,
    resp_v,
    decay_rate,
    norm_gain,
    prompt_cot,
    resp_cot,
):
    tok_count = prompt_q.shape[0]
    pair_count = resp_q.shape[0]
    resp_count = resp_q.shape[1]
    head_count = prompt_q.shape[1]
    head_size = prompt_q.shape[2]
    devices = lax.axis_size(CTX)
    position = lax.axis_index(CTX).astype(F32)
    features = head_count * lax.axis_size("head") * head_size
    zero_state = jnp.zeros((head_count, head_size, head_size), F32)
    zero_pair = jnp.zeros((pair_count, head_count, head_size, head_size), F32)
    prompt_span = jnp.exp(-decay_rate * tok_count)
    resp_span = jnp.exp(-decay_rate * resp_count)
    identity = (zero_state, jnp.ones_like(prompt_span), zero_pair, jnp.ones_like(resp_span))
    tail_weight = jnp.exp(-decay_rate * tok_count * (devices - 1.0 - position))[:, None, None]
    head_weight = jnp.exp(-decay_rate * resp_count * position)[:, None, None]

    def local_keys(keys, values):
        return key_state(keys, values, decay_rate, zero_state, BLK)

    def local_queries(queries, grads):
        return query_state(queries, grads, decay_rate, zero_state, BLK)

    def forward_one(queries, keys, values, carried):
        return chain_forward(queries, keys, values, carried, decay_rate, BLK)

    def backward_one(queries, keys, values, grads, entries, later):
        return chain_backward(queries, keys, values, grads, entries, later, decay_rate, BLK)

    prompt_local = local_keys(prompt_k, prompt_v)
    resp_local = jax.vmap(local_keys)(resp_k, resp_v)
    prompt_in, ignored, resp_part, unused = entering(
        (prompt_local, prompt_span, resp_local, resp_span), CTX, combine_all, identity, False
    )
    prompt_out, prompt_entries, end_state = chain_forward(
        prompt_q, prompt_k, prompt_v, prompt_in, decay_rate, BLK
    )
    final_state = broadcast(end_state, CTX, devices - 1)
    resp_in = resp_part + head_weight[None] * final_state[None]
    resp_out, resp_entries, resp_ends = jax.vmap(forward_one)(resp_q, resp_k, resp_v, resp_in)
    flat_out = resp_out.reshape((pair_count * resp_count, head_count, head_size))
    flat_cot = resp_cot.reshape((pair_count * resp_count, head_count, head_size))
    prompt_sq, prompt_inner = norm_sums(prompt_out, prompt_cot, norm_gain)
    resp_sq, resp_inner = norm_sums(flat_out, flat_cot, norm_gain)
    prompt_sq, prompt_inner, resp_sq, resp_inner = together(
        (prompt_sq, prompt_inner, resp_sq, resp_inner), "head"
    )
    prompt_y, prompt_grad = norm_finish(
        prompt_out, prompt_cot, norm_gain, prompt_sq, prompt_inner, features
    )
    resp_y, resp_grad = norm_finish(flat_out, flat_cot, norm_gain, resp_sq, resp_inner, features)
    resp_y = resp_y.reshape(resp_q.shape)
    resp_grad = resp_grad.reshape(resp_q.shape)
    prompt_later = local_queries(prompt_q, prompt_grad)
    resp_later = jax.vmap(local_queries)(resp_q, resp_grad)
    prompt_after, ignored_two, resp_after, unused_two = entering(
        (prompt_later, prompt_span, resp_later, resp_span), CTX, combine_all, identity, True
    )
    resp_dq, resp_dk, resp_dv, resp_start = jax.vmap(backward_one)(
        resp_q, resp_k, resp_v, resp_grad, resp_entries, resp_after
    )
    total_grad = broadcast(jnp.sum(resp_start, axis=0), CTX, 0)
    block_end = prompt_after + tail_weight * total_grad
    prompt_dq, prompt_dk, prompt_dv, unused_start = chain_backward(
        prompt_q, prompt_k, prompt_v, prompt_grad, prompt_entries, block_end, decay_rate, BLK
    )
    return (
        prompt_y,
        resp_y,
        prompt_dq.astype(BF16),
        prompt_dk.astype(BF16),
        prompt_dv.astype(BF16),
        resp_dq.astype(BF16),
        resp_dk.astype(BF16),
        resp_dv.astype(BF16),
    )


def solution(mesh):
    finer = Mesh(
        mesh.devices.reshape(4, 8, 2, mesh.shape["head"]), ("ctx_0", "ctx_1", "ctx_2", "head")
    )
    return jax.shard_map(
        shards,
        mesh=finer,
        in_specs=(
            P(CTX, "head", None),
            P(CTX, "head", None),
            P(CTX, "head", None),
            P(None, CTX, "head", None),
            P(None, CTX, "head", None),
            P(None, CTX, "head", None),
            P("head"),
            P("head", None),
            P(CTX, "head", None),
            P(None, CTX, "head", None),
        ),
        out_specs=(
            P(CTX, "head", None),
            P(None, CTX, "head", None),
            P(CTX, "head", None),
            P(CTX, "head", None),
            P(CTX, "head", None),
            P(None, CTX, "head", None),
            P(None, CTX, "head", None),
            P(None, CTX, "head", None),
        ),
        check_vma=False,
    )
```

profile of v0, /device:TPU:1, one launch (start us, length us, event | category | flops | bytes accessed | tf_op | source)
XLA Modules:
  0.0 558.3 jit_solution(6639252394930780137)
XLA Ops:
  7.3 0.9 copy.71
  8.2 0.9 copy.72
  9.1 1.2 multiply_exponential_fusion.10
  10.3 1.0 while.93
  11.7 2.1 concatenate.21
  13.9 29.9 %all-gather.27.cloned.1.call-done = f32[2,1154,128]{2,1,0:T(8,128)} async-done(((f32[1,1154,128]{2,1,0:T(8,128)}), f32[2,1154,128]{2,1,0:T(8,128)}) %all-gather.27.cloned.1.call-update) | async-done | bytes 1181712 | tf_op jit(solution)/shard_map/all_gather | solution.py:29
  43.8 0.8 fusion.239
  45.3 1.2 fusion.202
  46.5 1.4 fusion.160
  47.9 2.1 concatenate.22
  50.1 64.1 %all-gather.29.cloned.1.call-done = f32[8,1154,128]{2,1,0:T(8,128)} async-done(((f32[1,1154,128]{2,1,0:T(8,128)}), f32[8,1154,128]{2,1,0:T(8,128)}) %all-gather.29.cloned.1.call-update) | async-done | bytes 4726800 | tf_op jit(solution)/shard_map/all_gather | solution.py:29
  114.2 0.8 fusion.227
  117.0 1.9 fusion.200
  118.9 2.7 fusion.158
  121.7 2.1 concatenate.23
  123.9 0.8 fusion.238
  124.7 2.3 fusion.226
  127.0 37.2 %all-gather.31.cloned.1.call-done = f32[4,1154,128]{2,1,0:T(8,128)} async-done(((f32[1,1154,128]{2,1,0:T(8,128)}), f32[4,1154,128]{2,1,0:T(8,128)}) %all-gather.31.cloned.1.call-update) | async-done | bytes 2363408 | tf_op jit(solution)/shard_map/all_gather | solution.py:29
  164.2 0.8 fusion.231
  165.0 1.3 fusion.233
  166.3 1.7 multiply_add_fusion.1
  168.0 3.3 while.91
  168.4 0.9 fusion.349
  170.0 0.9 fusion.349
  172.4 0.9 convolution_bitcast_fusion.15
  173.3 1.0 fusion.237
  174.3 3.7 fusion.225
  179.0 1.0 fusion.182
  180.5 1.2 fusion.232
  181.7 91.5 %all-gather.23.cloned.1.call-done = f32[192,128,128]{2,1,0:T(8,128)} async-done(((f32[3,128,128]{2,1,0:T(8,128)}), f32[192,128,128]{2,1,0:T(8,128)}) %all-gather.23.cloned.1.call-update) | async-done | bytes 12582928 | tf_op jit(solution)/shard_map/all_gather | solution.py:54
  273.2 1.0 fusion.163
  274.4 3.5 add_convert_fusion
  279.0 9.9 %all-to-all-start = ((f32[12,1,512]{2,1,0:T(1,128)}), f32[12,1,512]{2,1,0:T(1,128)S(1)}, u32[]{:S(2)}, u32[]{:S(2)}) async-start(f32[12,1,512]{2,1,0:T(1,128)} %broadcast_in_dim.254), calls=%async_computation | async-start | bytes 49152 | tf_op jit(solution)/shard_map/all_to_all | solution.py:59
  289.0 9.2 %all-to-all-done = f32[12,1,512]{2,1,0:T(1,128)S(1)} async-done(((f32[12,1,512]{2,1,0:T(1,128)}), f32[12,1,512]{2,1,0:T(1,128)S(1)}, u32[]{:S(2)}, u32[]{:S(2)}) %all-to-all-start) | async-done | bytes 24608 | tf_op jit(solution)/shard_map/all_to_all | solution.py:59
  298.3 0.8 fusion.186
  299.1 1.0 while.94
  300.2 0.8 subtract_convert_fusion
  301.3 2.1 concatenate.25
  303.5 13.0 %all-gather.33.cloned.1.call-done = f32[2,1154,128]{2,1,0:T(8,128)} async-done(((f32[1,1154,128]{2,1,0:T(8,128)}), f32[2,1154,128]{2,1,0:T(8,128)}) %all-gather.33.cloned.1.call-update) | async-done | bytes 1181712 | tf_op jit(solution)/shard_map/all_gather | solution.py:29
  318.0 1.2 fusion.179
  319.2 1.4 fusion.144
  320.6 2.1 concatenate.26
  322.8 64.1 %all-gather.35.cloned.1.call-done = f32[8,1154,128]{2,1,0:T(8,128)} async-done(((f32[1,1154,128]{2,1,0:T(8,128)}), f32[8,1154,128]{2,1,0:T(8,128)}) %all-gather.35.cloned.1.call-update) | async-done | bytes 4726800 | tf_op jit(solution)/shard_map/all_gather | solution.py:29
  386.9 0.8 fusion.224
  390.3 1.9 fusion.177
  392.3 2.7 fusion.142
  395.0 2.1 concatenate.27
  397.3 0.9 fusion.235
  398.3 3.3 fusion.223
  401.6 35.9 %all-gather.37.cloned.1.call-done = f32[4,1154,128]{2,1,0:T(8,128)} async-done(((f32[1,1154,128]{2,1,0:T(8,128)}), f32[4,1154,128]{2,1,0:T(8,128)}) %all-gather.37.cloned.1.call-update) | async-done | bytes 2363408 | tf_op jit(solution)/shard_map/all_gather | solution.py:29
  437.6 1.5 fusion.228
  439.1 1.5 fusion.230
  440.8 1.6 add_reduce_fusion
  443.7 1.1 fusion.128
  444.8 1.1 convolution_bitcast_fusion.10
  446.3 1.5 fusion.124
  447.8 0.8 fusion.234
  448.7 1.6 fusion.222
  450.3 0.9 fusion.125
  451.2 0.8 fusion.126
  452.0 2.0 fusion.229
  454.0 89.5 %all-gather.25.cloned.1.call-done = f32[192,128,128]{2,1,0:T(8,128)} async-done(((f32[3,128,128]{2,1,0:T(8,128)}), f32[192,128,128]{2,1,0:T(8,128)}) %all-gather.25.cloned.1.call-update) | async-done | bytes 12582928 | tf_op jit(solution)/shard_map/all_gather | solution.py:54
  543.6 1.8 fusion.161
  545.5 4.0 while.92
  (413 shorter events, 22.3 us)
Async XLA Ops:
  7.2 4.2 copy-start
  7.2 4.2 copy-start.14
  7.2 36.6 %all-gather.27.cloned.1.call-start = ((), (), s32[]{:S(2)}) async-start(), calls=%async_computation.3 | async-start | bytes 1781760 | tf_op jit(solution)/shard_map/all_gather | solution.py:29
  11.3 38.7 %copy-start.27 = (f32[64,3]{0,1:T(4,128)}, f32[64,3]{0,1:T(4,128)S(1)}, u32[]{:S(2)}) copy-start(f32[64,3]{0,1:T(4,128)S(1)} %get-tuple-element.1068) | copy-start | bytes 2308
  11.3 289.7 %copy-start.29 = (f32[64,3]{0,1:T(4,128)}, f32[64,3]{0,1:T(4,128)S(1)}, u32[]{:S(2)}) copy-start(f32[64,3]{0,1:T(4,128)S(1)} %get-tuple-element.1067) | copy-start | bytes 2308
  13.8 100.4 %all-gather.29.cloned.1.call-start = ((), (), s32[]{:S(2)}) async-start(), calls=%async_computation.4 | async-start | bytes 5345280 | tf_op jit(solution)/shard_map/all_gather | solution.py:29
  44.6 71.1 %copy-start.97 = (f32[3]{0:T(128)}, f32[3]{0:T(128)S(1)}, u32[]{:S(2)}) copy-start(f32[3]{0:T(128)S(1)} %slice_bitcast_fusion.43) | copy-start | bytes 40
  50.0 114.2 %all-gather.31.cloned.1.call-start = ((), (), s32[]{:S(2)}) async-start(), calls=%async_computation.5 | async-start | bytes 2969600 | tf_op jit(solution)/shard_map/all_gather | solution.py:29
  115.0 6.6 %copy-start.99 = (f32[3]{0:T(128)}, f32[3]{0:T(128)S(1)}, u32[]{:S(2)}) copy-start(f32[3]{0:T(128)S(1)} %bitcast_multiply_fusion.12) | copy-start | bytes 40
  115.1 6.5 %copy-start.67 = (f32[3]{0:T(128)}, f32[3]{0:T(128)S(1)}, u32[]{:S(2)}) copy-start(f32[3]{0:T(128)S(1)} %get-tuple-element.1023) | copy-start | bytes 40
  115.1 6.5 %copy-start.69 = (f32[3]{0:T(128)}, f32[3]{0:T(128)S(1)}, u32[]{:S(2)}) copy-start(f32[3]{0:T(128)S(1)} %get-tuple-element.1024) | copy-start | bytes 40
  115.1 6.5 %copy-start.71 = (f32[3]{0:T(128)}, f32[3]{0:T(128)S(1)}, u32[]{:S(2)}) copy-start(f32[3]{0:T(128)S(1)} %get-tuple-element.1025) | copy-start | bytes 40
  115.1 6.5 %copy-start.73 = (f32[3]{0:T(128)}, f32[3]{0:T(128)S(1)}, u32[]{:S(2)}) copy-start(f32[3]{0:T(128)S(1)} %get-tuple-element.1026) | copy-start | bytes 40
  115.1 6.5 %copy-start.75 = (f32[3]{0:T(128)}, f32[3]{0:T(128)S(1)}, u32[]{:S(2)}) copy-start(f32[3]{0:T(128)S(1)} %get-tuple-element.1027) | copy-start | bytes 40
  115.1 6.5 %copy-start.77 = (f32[3]{0:T(128)}, f32[3]{0:T(128)S(1)}, u32[]{:S(2)}) copy-start(f32[3]{0:T(128)S(1)} %get-tuple-element.1028) | copy-start | bytes 40
  115.1 6.5 %copy-start.79 = (f32[3]{0:T(128)}, f32[3]{0:T(128)S(1)}, u32[]{:S(2)}) copy-start(f32[3]{0:T(128)S(1)} %get-tuple-element.1029) | copy-start | bytes 40
  118.9 5.0 copy-start.25
  118.9 5.0 copy-start.2
  123.8 149.4 %all-gather.23.cloned.1.call-start = ((), (), s32[]{:S(2)}) async-start(), calls=%async_computation.1 | async-start | bytes 12779520 | tf_op jit(solution)/shard_map/all_gather | solution.py:54
  168.0 4.1 copy-start.50
  168.0 4.2 copy-start.13
  172.2 5.8 %copy-start.17 = (f32[3,64,64]{2,1,0:T(8,128)}, f32[3,64,64]{2,1,0:T(8,128)S(1)}, u32[]{:S(2)}) copy-start(f32[3,64,64]{2,1,0:T(8,128)S(1)} %exponential_select_fusion.2) | copy-start | bytes 147460
  174.3 4.7 copy-start.26
  174.3 6.2 %copy-start.4 = (f32[4,1154,128]{2,1,0:T(8,128)S(1)}, f32[4,1154,128]{2,1,0:T(8,128)}, u32[]{:S(2)}) copy-start(f32[4,1154,128]{2,1,0:T(8,128)} %all-gather.31.cloned.1.call-done) | copy-start | bytes 7090180
  178.0 95.2 %copy-start.89 = (f32[3]{0:T(128)S(1)}, f32[3]{0:T(128)}, u32[]{:S(2)}) copy-start(f32[3]{0:T(128)} %get-tuple-element.1064) | copy-start | bytes 40
  178.0 96.2 %copy-start.68 = (f32[3]{0:T(128)S(1)}, f32[3]{0:T(128)}, u32[]{:S(2)}) copy-start(f32[3]{0:T(128)} %copy-done.67) | copy-start | bytes 40
  178.1 96.2 %copy-start.70 = (f32[3]{0:T(128)S(1)}, f32[3]{0:T(128)}, u32[]{:S(2)}) copy-start(f32[3]{0:T(128)} %copy-done.69) | copy-start | bytes 40
  178.1 96.2 %copy-start.72 = (f32[3]{0:T(128)S(1)}, f32[3]{0:T(128)}, u32[]{:S(2)}) copy-start(f32[3]{0:T(128)} %copy-done.71) | copy-start | bytes 40
  178.1 96.2 %copy-start.74 = (f32[3]{0:T(128)S(1)}, f32[3]{0:T(128)}, u32[]{:S(2)}) copy-start(f32[3]{0:T(128)} %copy-done.73) | copy-start | bytes 40
  178.1 96.2 %copy-start.76 = (f32[3]{0:T(128)S(1)}, f32[3]{0:T(128)}, u32[]{:S(2)}) copy-start(f32[3]{0:T(128)} %copy-done.75) | copy-start | bytes 40
  178.1 96.2 %copy-start.78 = (f32[3]{0:T(128)S(1)}, f32[3]{0:T(128)}, u32[]{:S(2)}) copy-start(f32[3]{0:T(128)} %copy-done.77) | copy-start | bytes 40
  178.1 96.2 %copy-start.80 = (f32[3]{0:T(128)S(1)}, f32[3]{0:T(128)}, u32[]{:S(2)}) copy-start(f32[3]{0:T(128)} %copy-done.79) | copy-start | bytes 40
  178.1 96.2 %copy-start.82 = (f32[3]{0:T(128)S(1)}, f32[3]{0:T(128)}, u32[]{:S(2)}) copy-start(f32[3]{0:T(128)} %copy-done.81) | copy-start | bytes 40
  178.1 96.2 %copy-start.98 = (f32[3]{0:T(128)S(1)}, f32[3]{0:T(128)}, u32[]{:S(2)}) copy-start(f32[3]{0:T(128)} %copy-done.97) | copy-start | bytes 40
  178.1 96.2 %copy-start.100 = (f32[3]{0:T(128)S(1)}, f32[3]{0:T(128)}, u32[]{:S(2)}) copy-start(f32[3]{0:T(128)} %copy-done.99) | copy-start | bytes 40
  178.1 96.2 %copy-start.101 = (f32[3]{0:T(128)S(1)}, f32[3]{0:T(128)}, u32[]{:S(2)}) copy-start(f32[3]{0:T(128)} %get-tuple-element.913) | copy-start | bytes 40
  178.2 96.2 %copy-start.102 = (f32[3]{0:T(128)S(1)}, f32[3]{0:T(128)}, u32[]{:S(2)}) copy-start(f32[3]{0:T(128)} %get-tuple-element.914) | copy-start | bytes 40
  180.5 93.8 %copy-start.103 = (f32[3]{0:T(128)S(1)}, f32[3]{0:T(128)}, u32[]{:S(2)}) copy-start(f32[3]{0:T(128)} %get-tuple-element.1045) | copy-start | bytes 40
  274.4 23.9 %copy-start.23 = (bf16[128,3,128]{2,0,1:T(8,128)(2,1)S(1)}, bf16[128,3,128]{2,0,1:T(8,128)(2,1)}, u32[]{:S(2)}) copy-start(bf16[128,3,128]{2,0,1:T(8,128)(2,1)} %param.26) | copy-start | bytes 294916
  279.0 19.2 %all-to-all-start = ((f32[12,1,512]{2,1,0:T(1,128)}), f32[12,1,512]{2,1,0:T(1,128)S(1)}, u32[]{:S(2)}, u32[]{:S(2)}) async-start(f32[12,1,512]{2,1,0:T(1,128)} %broadcast_in_dim.254), calls=%async_computation | async-start | bytes 49152 | tf_op jit(solution)/shard_map/all_to_all | solution.py:59
  288.9 27.6 %all-gather.33.cloned.1.call-start = ((), (), s32[]{:S(2)}) async-start(), calls=%async_computation.6 | async-start | bytes 1781760 | tf_op jit(solution)/shard_map/all_gather | solution.py:29
  303.5 83.4 %all-gather.35.cloned.1.call-start = ((), (), s32[]{:S(2)}) async-start(), calls=%async_computation.7 | async-start | bytes 5345280 | tf_op jit(solution)/shard_map/all_gather | solution.py:29
  317.3 70.4 %copy-start.90 = (f32[3]{0:T(128)}, f32[3]{0:T(128)S(1)}, u32[]{:S(2)}) copy-start(f32[3]{0:T(128)S(1)} %slice_bitcast_fusion.22) | copy-start | bytes 40
  322.7 114.8 %all-gather.37.cloned.1.call-start = ((), (), s32[]{:S(2)}) async-start(), calls=%async_computation.8 | async-start | bytes 2969600 | tf_op jit(solution)/shard_map/all_gather | solution.py:29
  392.3 5.1 copy-start.3
  397.1 146.4 %all-gather.25.cloned.1.call-start = ((), (), s32[]{:S(2)}) async-start(), calls=%async_computation.2 | async-start | bytes 12779520 | tf_op jit(solution)/shard_map/all_gather | solution.py:54
  446.1 4.1 copy-start.30
  446.1 4.2 copy-start.28
  448.6 94.9 %copy-start.52 = (f32[3]{0:T(128)S(1)}, f32[3]{0:T(128)}, u32[]{:S(2)}) copy-start(f32[3]{0:T(128)} %copy-done.51) | copy-start | bytes 40
  448.6 94.9 %copy-start.54 = (f32[3]{0:T(128)S(1)}, f32[3]{0:T(128)}, u32[]{:S(2)}) copy-start(f32[3]{0:T(128)} %copy-done.53) | copy-start | bytes 40
  448.6 94.9 %copy-start.56 = (f32[3]{0:T(128)S(1)}, f32[3]{0:T(128)}, u32[]{:S(2)}) copy-start(f32[3]{0:T(128)} %copy-done.55) | copy-start | bytes 40
  448.6 94.9 %copy-start.58 = (f32[3]{0:T(128)S(1)}, f32[3]{0:T(128)}, u32[]{:S(2)}) copy-start(f32[3]{0:T(128)} %copy-done.57) | copy-start | bytes 40
  448.6 94.9 %copy-start.60 = (f32[3]{0:T(128)S(1)}, f32[3]{0:T(128)}, u32[]{:S(2)}) copy-start(f32[3]{0:T(128)} %copy-done.59) | copy-start | bytes 40
  448.6 94.9 %copy-start.62 = (f32[3]{0:T(128)S(1)}, f32[3]{0:T(128)}, u32[]{:S(2)}) copy-start(f32[3]{0:T(128)} %copy-done.61) | copy-start | bytes 40
  448.6 94.9 %copy-start.64 = (f32[3]{0:T(128)S(1)}, f32[3]{0:T(128)}, u32[]{:S(2)}) copy-start(f32[3]{0:T(128)} %copy-done.63) | copy-start | bytes 40
  448.6 94.9 %copy-start.66 = (f32[3]{0:T(128)S(1)}, f32[3]{0:T(128)}, u32[]{:S(2)}) copy-start(f32[3]{0:T(128)} %copy-done.65) | copy-start | bytes 40
  448.6 94.9 %copy-start.91 = (f32[3]{0:T(128)S(1)}, f32[3]{0:T(128)}, u32[]{:S(2)}) copy-start(f32[3]{0:T(128)} %copy-done.90) | copy-start | bytes 40
  448.7 94.9 %copy-start.92 = (f32[3]{0:T(128)S(1)}, f32[3]{0:T(128)}, u32[]{:S(2)}) copy-start(f32[3]{0:T(128)} %get-tuple-element.903) | copy-start | bytes 40
  448.7 94.9 %copy-start.93 = (f32[3]{0:T(128)S(1)}, f32[3]{0:T(128)}, u32[]{:S(2)}) copy-start(f32[3]{0:T(128)} %get-tuple-element.904) | copy-start | bytes 40
  448.7 94.9 %copy-start.95 = (f32[3]{0:T(128)S(1)}, f32[3]{0:T(128)}, u32[]{:S(2)}) copy-start(f32[3]{0:T(128)} %copy-done.94) | copy-start | bytes 40
  448.7 94.9 %copy-start.96 = (f32[3]{0:T(128)S(1)}, f32[3]{0:T(128)}, u32[]{:S(2)}) copy-start(f32[3]{0:T(128)} %get-tuple-element.1059) | copy-start | bytes 40
  452.0 93.4 %copy-start.16 = (bf16[2,3,128,128]{3,2,1,0:T(8,128)(2,1)S(1)}, bf16[2,3,128,128]{3,2,1,0:T(8,128)(2,1)}, u32[]{:S(2)}) copy-start(bf16[2,3,128,128]{3,2,1,0:T(8,128)(2,1)} %copy-done.15) | copy-start | bytes 589828
  452.0 93.4 %copy-start.21 = (bf16[2,64,3,128]{3,1,2,0:T(8,128)(2,1)S(1)}, bf16[2,64,3,128]{3,1,2,0:T(8,128)(2,1)}, u32[]{:S(2)}) copy-start(bf16[2,64,3,128]{3,1,2,0:T(8,128)(2,1)} %copy.131) | copy-start | bytes 294916
  452.0 93.4 %copy-start.22 = (bf16[2,64,3,128]{3,1,2,0:T(8,128)(2,1)S(1)}, bf16[2,64,3,128]{3,1,2,0:T(8,128)(2,1)}, u32[]{:S(2)}) copy-start(bf16[2,64,3,128]{3,1,2,0:T(8,128)(2,1)} %copy.130) | copy-start | bytes 294916
  (50 other events, 122.4 us)
Sparse Core Ops, SparseCore 0:
  13.9 29.8 all-gather.26
  50.1 64.0 all-gather.28
  123.9 40.2 all-gather.30
  172.2 100.9 all-gather.22
  303.6 12.8 all-gather.32
  322.8 64.0 all-gather.34
  397.2 40.2 all-gather.36
  442.5 100.9 all-gather.24
where the time goes:
time: 559 us; the launch traced here: 558 us
  waiting for transfers between devices  435 us (78%)
  local copies, waits for them, and re-layouts  50 us (9%)
  other arithmetic  31.2 us (6%)
  between operations  16 us (3%)
  matrix products  15.7 us (3%)
  starting transfers between devices  10.4 us (2%)
    all_gather x6, waiting for transfers between devices, gathered_once(): both, at, found = (lax.all_gather(jnp.concatenate(lines), axis), 0, {})  244 us
    all_gather x2, waiting for transfers between devices, broadcast(): lax.all_gather(x, axis)  181 us
    slice x12, local copies, waits for them, and re-layouts, entering(): subtotal = combine(subtotal, jax.tree.map(lambda part: part[k], pieces))  20.3 us
    dot_general x38, matrix products, contract(): return jnp.einsum(form, left, right, preferred_element_type=F32)  15.7 us
    concatenate x6, local copies, waits for them, and re-layouts, gathered_once(): both, at, found = (lax.all_gather(jnp.concatenate(lines), axis), 0, {})  12.6 us
  transfers between devices with their start and end apart: 9, of which 9 were waited for; matrix products, arithmetic and copies ran while one was open for 5% of the time, Pallas kernels for 0%

commit v1 on v0

v1 whole, which is shorter than its diff:
```python
import functools

import jax
import jax.numpy as jnp
from jax import lax
from jax.experimental import pallas as pl
from jax.experimental.pallas import tpu as pltpu
from jax.sharding import PartitionSpec as P

GRID = (4, 8, 2)
MESH = pl.DeviceIdType.MESH
F32 = jnp.float32
BF16 = jnp.bfloat16


def dot(left, right, dims):
    return lax.dot_general(left, right, (dims, ((), ())), preferred_element_type=F32)


def dot_nn(left, right):
    return dot(left, right, ((1,), (0,)))


def dot_nt(left, right):
    return dot(left, right, ((1,), (1,)))


def dot_tn(left, right):
    return dot(left, right, ((0,), (0,)))


class Place:
    def __init__(self, grid, reverse):
        self.nx, self.ny, _ = grid
        self.reverse = reverse
        ctx = lax.axis_index("ctx")
        self.head = lax.axis_index("head")
        self.core = lax.rem(ctx, 2)
        self.phys_y = lax.rem(ctx // 2, self.ny)
        self.phys_x = ctx // (2 * self.ny)
        self.y = self.ny - 1 - self.phys_y if reverse else self.phys_y
        self.x = self.nx - 1 - self.phys_x if reverse else self.phys_x
        self.order = 1 - self.core if reverse else self.core

    def device(self, x, y, core):
        return ((x * self.ny + y) * 2 + core, self.head)

    def partner(self):
        return self.device(self.phys_x, self.phys_y, 1 - self.core)

    def along_y(self, y):
        return self.device(self.phys_x, self.ny - 1 - y if self.reverse else y, self.core)

    def along_x(self, x):
        return self.device(self.nx - 1 - x if self.reverse else x, self.phys_y, self.core)


class Scan:
    def __init__(self, way, place, rate, lengths, refs, pending):
        self.way, self.place, self.rate, self.lengths = way, place, rate, lengths
        (self.loc, self.pair, self.csend, self.a1, self.tx, self.psend, self.a2, self.fsend, self.st) = refs[:9]
        (self.c_s, self.c_r, self.a1_s, self.a1_r, self.x_s, self.x_r, self.a2_s, self.a2_r, self.f_s, self.f_r) = refs[9:]
        self.pending = pending
        self.rows = self.csend.shape[4]
        self.half = self.fsend.shape[3]

    def decay(self, h, tokens):
        return jnp.exp(jnp.full((1, 128), -self.rate[h], F32) * tokens)

    def copy(self, src, dst, send, recv, device):
        return pltpu.make_async_remote_copy(
            src_ref=src, dst_ref=dst, send_sem=send, recv_sem=recv, device_id=device, device_id_type=MESH
        )

    def start(self, copy):
        copy.start()
        self.pending.append(copy)

    def own_half(self):
        return pl.ds(pl.multiple_of(self.place.core * self.half, self.half), self.half)

    def pair_copy(self, h):
        w, p = self.way, self.place
        other = pl.ds(pl.multiple_of((1 - p.core) * self.half, self.half), self.half)
        return self.copy(
            self.loc.at[w, h, :, other, :], self.pair.at[w, h], self.c_s.at[w, h], self.c_r.at[w, h], p.partner()
        )

    def start_pair(self, h):
        self.start(self.pair_copy(h))

    def first_second(self, h, s):
        own = self.loc[self.way, h, s, self.own_half(), :]
        other = self.pair[self.way, h, s]
        leads = self.place.order == 0
        return jnp.where(leads, own, other), jnp.where(leads, other, own)

    def gather_copy(self, h, k):
        w, p = self.way, self.place
        to = lax.rem(p.y + k, p.ny)
        return self.copy(
            self.csend.at[w, h, to], self.a1.at[w, h, p.y], self.a1_s.at[w, h, k], self.a1_r.at[w, h, p.y], p.along_y(to)
        )

    def chip(self, h):
        w, p = self.way, self.place
        self.pair_copy(h).wait_recv()
        for s, length in enumerate(self.lengths):
            first, second = self.first_second(h, s)
            both = self.decay(h, float(length)) * first + second
            for j in range(p.ny):
                self.csend[w, h, j, s] = both[j * self.rows : (j + 1) * self.rows]
        self.a1[w, h, p.y] = self.csend[w, h, p.y]
        for k in far_first(p.ny):
            self.start(self.gather_copy(h, k))

    def wait_along(self, buf, sem, here, n, h, device):
        w = self.way
        for k in range(1, n):
            source = lax.rem(here + k, n)
            self.copy(
                buf.at[w, h, source], buf.at[w, h, source], sem.at[w, h, source], sem.at[w, h, source], device(source)
            ).wait_recv()

    def column(self, h):
        w, p = self.way, self.place
        self.wait_along(self.a1, self.a1_r, p.y, p.ny, h, p.along_y)
        for s, length in enumerate(self.lengths):
            step = self.decay(h, 2.0 * length)
            total = self.a1[w, h, 0, s]
            for j in range(1, p.ny):
                total = step * total + self.a1[w, h, j, s]
            self.tx[w, h, p.x, s] = total
        for k in far_first(p.nx):
            to = lax.rem(p.x + k, p.nx)
            self.start(
                self.copy(
                    self.tx.at[w, h, p.x], self.tx.at[w, h, p.x], self.x_s.at[w, h, k], self.x_r.at[w, h, p.x], p.along_x(to)
                )
            )

    def spread(self, h, sources, targets):
        w, p = self.way, self.place
        self.wait_along(self.tx, self.x_r, p.x, p.nx, h, p.along_x)
        bases, totals = [], []
        for s, length in enumerate(self.lengths):
            step = self.decay(h, 2.0 * length * p.ny)
            run = self.tx[w, h, 0, s]
            base = jnp.zeros_like(run)
            for j in range(1, p.nx):
                base = jnp.where(p.x == j, run, base)
                run = step * run + self.tx[w, h, j, s]
            bases.append(base)
            totals.append(run)
        given = sum(totals[s] for s in sources)
        for s in targets:
            before = (p.x * (2 * p.ny * self.lengths[s])).astype(F32)
            bases[s] = bases[s] + self.decay(h, before) * given
        for s, length in enumerate(self.lengths):
            step = self.decay(h, 2.0 * length)
            entry = bases[s]
            for j in range(p.ny):
                self.psend[w, h, j, s] = entry
                if j < p.ny - 1:
                    entry = step * entry + self.a1[w, h, j, s]
        self.a2[w, h, p.y] = self.psend[w, h, p.y]
        for k in far_first(p.ny):
            to = lax.rem(p.y + k, p.ny)
            self.start(
                self.copy(
                    self.psend.at[w, h, to], self.a2.at[w, h, p.y], self.a2_s.at[w, h, k], self.a2_r.at[w, h, p.y], p.along_y(to)
                )
            )

    def final_copy(self, h):
        w, p = self.way, self.place
        return self.copy(
            self.fsend.at[w, h], self.st.at[w, h, :, self.own_half(), :], self.f_s.at[w, h], self.f_r.at[w, h], p.partner()
        )

    def finish(self, h):
        w, p = self.way, self.place
        self.wait_along(self.a2, self.a2_r, p.y, p.ny, h, p.along_y)
        leads = p.order == 0
        for s, length in enumerate(self.lengths):
            entry = jnp.concatenate([self.a2[w, h, j, s] for j in range(p.ny)], axis=0)
            first, _ = self.first_second(h, s)
            after = self.decay(h, float(length)) * entry + first
            self.st[w, h, s, self.own_half(), :] = jnp.where(leads, entry, after)
            self.fsend[w, h, s] = jnp.where(leads, after, entry)
        self.start(self.final_copy(h))

    def ready(self, h):
        w, p = self.way, self.place
        other = pl.ds(pl.multiple_of((1 - p.core) * self.half, self.half), self.half)
        landed = self.st.at[w, h, :, other, :]
        self.copy(landed, landed, self.f_r.at[w, h], self.f_r.at[w, h], p.partner()).wait_recv()

    def exchange(self, heads, sources, targets):
        for h in range(heads + 1):
            if h < heads:
                self.column(h)
            if h > 0:
                self.spread(h - 1, sources, targets)
        for h in range(heads):
            self.finish(h)


def far_first(n):
    return sorted(range(1, n), key=lambda k: -min(k, n - k))


def column_of(row):
    return jnp.broadcast_to(row, (128, 128)).T


def kernel(
    grid, nz, rate, gain, pq, pk, pv, pc, rq, rk, rv, rc,
    py, ry, pdq, pdk, pdv, rdq, rdk, rdv,
    loc, pair, csend, a1, tx, psend, a2, fsend, st, stat, pmix, rmix, pout, rout, pgrad, rgrad, dk_p, dv_p, dk_r, dv_r,
    c_s, c_r, a1_s, a1_r, x_s, x_r, a2_s, a2_r, f_s, f_r, z_s, z_r,
):
    heads, tokens, width = pq.shape
    count = rq.shape[2]
    features = float(heads * nz * width)
    ahead, back = Place(grid, False), Place(grid, True)
    ctx, z = lax.axis_index("ctx"), ahead.head

    barrier = pltpu.get_barrier_semaphore()
    peers = [ahead.partner()]
    peers += [ahead.along_y(lax.rem(ahead.y + k, grid[1])) for k in range(1, grid[1])]
    peers += [ahead.along_x(lax.rem(ahead.x + k, grid[0])) for k in range(1, grid[0])]
    peers += [(ctx, lax.rem(z + k, nz)) for k in range(1, nz)]
    for peer in peers:
        pl.semaphore_signal(barrier, inc=1, device_id=peer, device_id_type=MESH)

    pending = []
    refs = (loc, pair, csend, a1, tx, psend, a2, fsend, st, c_s, c_r, a1_s, a1_r, x_s, x_r, a2_s, a2_r, f_s, f_r)
    lengths = (tokens, count, count)
    fwd = Scan(0, ahead, rate, lengths, refs, pending)
    bwd = Scan(1, back, rate, lengths, refs, pending)

    row = lax.broadcasted_iota(jnp.int32, (128, 128), 0)
    col = lax.broadcasted_iota(jnp.int32, (128, 128), 1)
    lag = (row - col).astype(F32)
    causal = row >= col
    apart = (row // count) != (col // count)
    place_p = row.astype(F32)
    place_r = lax.rem(row, count).astype(F32)

    def power(h, steps):
        return jnp.exp(jnp.full((128, 128), -rate[h], F32) * steps)

    def pairs(ref, h):
        return jnp.concatenate([ref[0, h], ref[1, h]], axis=0)

    def masks(h):
        mask = jnp.where(causal, power(h, jnp.maximum(lag, 0.0)), 0.0)
        return mask, jnp.where(apart, 0.0, mask)

    for h in range(heads):
        keys = (pk[h].astype(F32) * power(h, tokens - 1.0 - place_p)).astype(BF16)
        loc[0, h, 0] = dot_tn(keys, pv[h])
        keys = (pairs(rk, h).astype(F32) * power(h, count - 1.0 - place_r)).astype(BF16)
        for r in range(2):
            loc[0, h, 1 + r] = dot_tn(keys[r * count : (r + 1) * count], rv[r, h])
    pl.semaphore_wait(barrier, len(peers))
    for h in range(heads):
        fwd.start_pair(h)
    for h in range(heads):
        fwd.chip(h)

    for h in range(heads):
        mask_p, mask_r = masks(h)
        pmix[h] = (dot_nt(pq[h], pk[h]) * mask_p).astype(BF16)
        rmix[h] = (dot_nt(pairs(rq, h), pairs(rk, h)) * mask_r).astype(BF16)
        pout[h] = dot_nn(pmix[h], pv[h])
        rout[h] = dot_nn(rmix[h], pairs(rv, h))

    fwd.exchange(heads, (0,), (1, 2))

    sums = [jnp.zeros((128, 128), F32) for _ in range(4)]
    for h in range(heads):
        fwd.ready(h)
        out = pout[h] + power(h, place_p + 1.0) * dot_nn(pq[h], st[0, h, 0].astype(BF16))
        pout[h] = out
        sums[0] += out * out
        sums[1] += gain[h : h + 1] * pc[h].astype(F32) * out
        across = [dot_nn(rq[r, h], st[0, h, 1 + r].astype(BF16)) for r in range(2)]
        out = rout[h] + power(h, place_r + 1.0) * jnp.concatenate(across, axis=0)
        rout[h] = out
        sums[2] += out * out
        sums[3] += gain[h : h + 1] * pairs(rc, h).astype(F32) * out
    lines = [jnp.sum(part.T, axis=0, keepdims=True) for part in sums]
    stat[z] = jnp.concatenate(lines + [jnp.zeros((4, 128), F32)], axis=0)

    for k in far_first(nz):
        to = (ctx, lax.rem(z + k, nz))
        fwd.start(fwd.copy(stat.at[z], stat.at[z], z_s.at[k], z_r.at[z], to))
    for k in range(1, nz):
        source = lax.rem(z + k, nz)
        fwd.copy(stat.at[source], stat.at[source], z_r.at[source], z_r.at[source], (ctx, source)).wait_recv()
    total = stat[0]
    for k in range(1, nz):
        total = total + stat[k]

    def norms(at):
        inv = lax.rsqrt(total[at : at + 1] / features + 1e-05)
        return column_of(inv), column_of(total[at + 1 : at + 2] * inv * inv * inv / features)

    inv_p, coef_p = norms(0)
    inv_r, coef_r = norms(2)
    for h in range(heads):
        grad = (gain[h : h + 1] * pc[h].astype(F32) * inv_p - pout[h] * coef_p).astype(BF16)
        pgrad[h] = grad
        queries = (pq[h].astype(F32) * power(h, place_p + 1.0)).astype(BF16)
        loc[1, h, 0] = dot_tn(queries, grad)
        grad = (gain[h : h + 1] * pairs(rc, h).astype(F32) * inv_r - rout[h] * coef_r).astype(BF16)
        rgrad[h] = grad
        queries = (pairs(rq, h).astype(F32) * power(h, place_r + 1.0)).astype(BF16)
        for r in range(2):
            part = slice(r * count, (r + 1) * count)
            loc[1, h, 1 + r] = dot_tn(queries[part], grad[part])
        bwd.start_pair(h)
    for h in range(heads):
        bwd.chip(h)

    for h in range(heads):
        py[h] = (gain[h : h + 1] * pout[h] * inv_p).astype(BF16)
        normed = (gain[h : h + 1] * rout[h] * inv_r).astype(BF16)
        mask_p, mask_r = masks(h)
        grad = pgrad[h]
        dmix = (dot_nt(grad, pv[h]) * mask_p).astype(BF16)
        across = dot_nt(grad, st[0, h, 0].astype(BF16))
        pdq[h] = (dot_nn(dmix, pk[h]) + power(h, place_p + 1.0) * across).astype(BF16)
        dk_p[h] = dot_tn(dmix, pq[h])
        dv_p[h] = dot_tn(pmix[h], grad)
        grad = rgrad[h]
        dmix = (dot_nt(grad, pairs(rv, h)) * mask_r).astype(BF16)
        across = [dot_nt(grad[r * count : (r + 1) * count], st[0, h, 1 + r].astype(BF16)) for r in range(2)]
        queries = dot_nn(dmix, pairs(rk, h)) + power(h, place_r + 1.0) * jnp.concatenate(across, axis=0)
        dk_r[h] = dot_tn(dmix, pairs(rq, h))
        dv_r[h] = dot_tn(rmix[h], grad)
        for r in range(2):
            part = slice(r * count, (r + 1) * count)
            ry[r, h] = normed[part]
            rdq[r, h] = queries[part].astype(BF16)

    bwd.exchange(heads, (1, 2), (0,))

    for h in range(heads):
        bwd.ready(h)
        later = st[1, h, 0].astype(BF16)
        fade = power(h, tokens - 1.0 - place_p)
        pdk[h] = (dk_p[h] + fade * dot_nt(pv[h], later)).astype(BF16)
        pdv[h] = (dv_p[h] + fade * dot_nn(pk[h], later)).astype(BF16)
        fade = power(h, count - 1.0 - place_r)
        for r in range(2):
            part = slice(r * count, (r + 1) * count)
            later = st[1, h, 1 + r].astype(BF16)
            rdk[r, h] = (dk_r[h, part, :] + fade[part] * dot_nt(rv[r, h], later)).astype(BF16)
            rdv[r, h] = (dv_r[h, part, :] + fade[part] * dot_nn(rk[r, h], later)).astype(BF16)

    for copy in pending:
        copy.wait_send()


def shards(grid, nz, prompt_q, prompt_k, prompt_v, resp_q, resp_k, resp_v, decay_rate, norm_gain, prompt_cot, resp_cot):
    nx, ny, _ = grid
    tokens, heads, width = prompt_q.shape
    count = resp_q.shape[1]
    half, rows = width // 2, width // 2 // ny
    prompt = [jnp.transpose(a, (1, 0, 2)) for a in (prompt_q, prompt_k, prompt_v, prompt_cot)]
    resp = [jnp.transpose(a, (0, 2, 1, 3)) for a in (resp_q, resp_k, resp_v, resp_cot)]
    flat = jax.ShapeDtypeStruct((heads, tokens, width), BF16)
    duo = jax.ShapeDtypeStruct((2, heads, count, width), BF16)
    vmem = pl.BlockSpec(memory_space=pltpu.VMEM)
    block = (heads, tokens, width)
    scratch = [
        pltpu.VMEM((2, heads, 3, width, width), F32),
        pltpu.VMEM((2, heads, 3, half, width), F32),
        pltpu.VMEM((2, heads, ny, 3, rows, width), F32),
        pltpu.VMEM((2, heads, ny, 3, rows, width), F32),
        pltpu.VMEM((2, heads, nx, 3, rows, width), F32),
        pltpu.VMEM((2, heads, ny, 3, rows, width), F32),
        pltpu.VMEM((2, heads, ny, 3, rows, width), F32),
        pltpu.VMEM((2, heads, 3, half, width), F32),
        pltpu.VMEM((2, heads, 3, width, width), F32),
        pltpu.VMEM((nz, 8, width), F32),
        pltpu.VMEM(block, BF16),
        pltpu.VMEM(block, BF16),
        pltpu.VMEM(block, F32),
        pltpu.VMEM(block, F32),
        pltpu.VMEM(block, BF16),
        pltpu.VMEM(block, BF16),
        pltpu.VMEM(block, F32),
        pltpu.VMEM(block, F32),
        pltpu.VMEM(block, F32),
        pltpu.VMEM(block, F32),
    ]
    dma = pltpu.SemaphoreType.DMA
    scratch += [dma((2, heads))] * 2 + [dma((2, heads, ny))] * 2 + [dma((2, heads, nx))] * 2
    scratch += [dma((2, heads, ny))] * 2 + [dma((2, heads))] * 2 + [dma((nz,))] * 2
    out = pl.pallas_call(
        functools.partial(kernel, grid, nz),
        out_shape=(flat, duo, flat, flat, flat, duo, duo, duo),
        in_specs=[pl.BlockSpec(memory_space=pltpu.SMEM)] + [vmem] * 9,
        out_specs=(vmem,) * 8,
        scratch_shapes=scratch,
        compiler_params=pltpu.CompilerParams(collective_id=0, has_side_effects=True),
    )(decay_rate, norm_gain, *prompt, *resp)
    return tuple(
        jnp.transpose(a, (1, 0, 2)) if a.ndim == 3 else jnp.transpose(a, (0, 2, 1, 3)) for a in out
    )


def solution(mesh):
    flat, duo = P("ctx", "head", None), P(None, "ctx", "head", None)
    return jax.shard_map(
        functools.partial(shards, GRID, mesh.shape["head"]),
        mesh=mesh,
        in_specs=(flat, flat, flat, duo, duo, duo, P("head"), P("head", None), flat, duo),
        out_specs=(flat, duo, flat, flat, flat, duo, duo, duo),
        check_vma=False,
    )
```

time: 559 us -> 79.8 us (0.14)
  waiting for transfers between devices: 435 us -> 0 us
  Pallas kernels: 0 us -> 71 us
  local copies, waits for them, and re-layouts: 50 us -> 7.79 us
  other arithmetic: 31.2 us -> 0 us
  matrix products: 15.7 us -> 0 us
  between operations: 16 us -> 0.66 us
  starting transfers between devices: 10.4 us -> 0 us
    all_gather x8 -> x0, waiting for transfers between devices: 425 us -> none  [the longest x6 244 us: gathered_once(): both, at, found = (lax.all_gather(jnp.concatenate(lines), axis), 0, {})]
    pallas_call x0 -> x1, Pallas kernels: none -> 71 us  [shards(): pl.pallas_call(functools.partial(kernel, grid, nz), out_shape=(flat, duo,...]
    slice x18 -> x0, local copies, waits for them, and re-layouts: 25.8 us -> none  [the longest x12 20.3 us: entering(): subtotal = combine(subtotal, jax.tree.map(lambda part: part[k], pieces))]
    add x16 -> x0, other arithmetic: 18.9 us -> none  [the longest x4 8.12 us: combine_all(): later[2] + later[3][:, None, None] * earlier[2]]
    dot_general x38 -> x0, matrix products: 15.7 us -> none  [contract(): return jnp.einsum(form, left, right, preferred_element_type=F32)]
    concatenate x6 -> x0, local copies, waits for them, and re-layouts: 12.6 us -> none  [gathered_once(): both, at, found = (lax.all_gather(jnp.concatenate(lines), axis), 0, {})]
    all_to_all x1 -> x0, starting transfers between devices: 9.9 us -> none  [from_everyone(): return lax.all_to_all(copies, axis, split_axis=0, concat_axis=0, tiled=True)]
    all_to_all x1 -> x0, waiting for transfers between devices: 9.23 us -> none  [from_everyone(): return lax.all_to_all(copies, axis, split_axis=0, concat_axis=0, tiled=True)]
  transfers between devices with their start and end apart: 9 -> 0, of which waited for: 9 -> 0; matrix products, arithmetic and copies ran while one was open for 5% -> 0% of each run, Pallas kernels for 0% -> 0%
where the time goes in v1:
time: 79.8 us; the launch traced here: 79.4 us
  Pallas kernels  71 us (89%)
  local copies, waits for them, and re-layouts  7.79 us (10%)
    pallas_call x1, Pallas kernels, shards(): pl.pallas_call(functools.partial(kernel, grid, nz), out_shape=(flat, duo,...  71 us
    unnamed x22, local copies, waits for them, and re-layouts  7.79 us

profile of v1, /device:TPU:1, one launch (start us, length us, event | category | flops | bytes accessed | tf_op | source)
XLA Modules:
  0.0 79.4 jit_solution(17284182844953643605)
XLA Ops:
  0.6 71.0 %shard_map.161 = (bf16[3,128,128]{2,1,0:T(8,128)(2,1)}, bf16[2,3,64,128]{3,2,1,0:T(8,128)(2,1)}, bf16[3,128,128]{2,1,0:T(8,128)(2,1)}, bf16[3,128,128]{2,1,0:T(8...) custom-call(f32[3]{0:T(128)} %rate.1, ...), custom_call_target="tpu_custom_call" | custom-call | tf_op jit(solution)/shard_map/pallas_call | solution.py:404
  71.6 0.0 copy-start.6
  71.6 1.6 %copy.26 = bf16[128,3,128]{2,0,1:T(8,128)(2,1)} copy(bf16[128,3,128]{2,0,1:T(8,128)(2,1)} %bitcast.23) | data formatting | bytes 196608
  73.2 0.0 copy-done.6
  73.2 0.0 copy-start.5
  73.2 0.6 copy.27
  73.8 0.3 copy-done.5
  74.1 0.0 copy-start.4
  74.1 0.6 copy.28
  74.8 0.3 copy-done.4
  75.0 0.0 copy-start.3
  75.0 0.6 copy.29
  75.7 0.3 copy-done.3
  76.0 0.0 copy-start.2
  76.0 0.6 copy.30
  76.6 0.3 copy-done.2
  76.9 0.0 copy-start.1
  76.9 0.6 copy.31
  77.5 0.3 copy-done.1
  77.8 0.0 copy-start
  77.8 0.6 copy.32
  78.5 0.3 copy-done
  78.8 0.6 copy.33
Async XLA Ops:
  71.6 1.6 %copy-start.6 = (bf16[2,3,64,128]{3,2,1,0:T(8,128)(2,1)S(1)}, bf16[2,3,64,128]{3,2,1,0:T(8,128)(2,1)}, u32[]{:S(2)}) copy-start(bf16[2,3,64,128]{3,2,1,0:T(8,128)(2,1)} %get-tuple-element.17) | copy-start | bytes 294916
  73.2 0.9 %copy-start.5 = (bf16[3,128,128]{2,1,0:T(8,128)(2,1)S(1)}, bf16[3,128,128]{2,1,0:T(8,128)(2,1)}, u32[]{:S(2)}) copy-start(bf16[3,128,128]{2,1,0:T(8,128)(2,1)} %get-tuple-element.18) | copy-start | bytes 294916
  74.1 0.9 %copy-start.4 = (bf16[3,128,128]{2,1,0:T(8,128)(2,1)S(1)}, bf16[3,128,128]{2,1,0:T(8,128)(2,1)}, u32[]{:S(2)}) copy-start(bf16[3,128,128]{2,1,0:T(8,128)(2,1)} %get-tuple-element.19) | copy-start | bytes 294916
  75.0 0.9 %copy-start.3 = (bf16[3,128,128]{2,1,0:T(8,128)(2,1)S(1)}, bf16[3,128,128]{2,1,0:T(8,128)(2,1)}, u32[]{:S(2)}) copy-start(bf16[3,128,128]{2,1,0:T(8,128)(2,1)} %get-tuple-element.20) | copy-start | bytes 294916
  76.0 0.9 %copy-start.2 = (bf16[2,3,64,128]{3,2,1,0:T(8,128)(2,1)S(1)}, bf16[2,3,64,128]{3,2,1,0:T(8,128)(2,1)}, u32[]{:S(2)}) copy-start(bf16[2,3,64,128]{3,2,1,0:T(8,128)(2,1)} %get-tuple-element.21) | copy-start | bytes 294916
  76.9 0.9 %copy-start.1 = (bf16[2,3,64,128]{3,2,1,0:T(8,128)(2,1)S(1)}, bf16[2,3,64,128]{3,2,1,0:T(8,128)(2,1)}, u32[]{:S(2)}) copy-start(bf16[2,3,64,128]{3,2,1,0:T(8,128)(2,1)} %get-tuple-element.22) | copy-start | bytes 294916
  77.8 0.9 %copy-start = (bf16[2,3,64,128]{3,2,1,0:T(8,128)(2,1)S(1)}, bf16[2,3,64,128]{3,2,1,0:T(8,128)(2,1)}, u32[]{:S(2)}) copy-start(bf16[2,3,64,128]{3,2,1,0:T(8,128)(2,1)} %get-tuple-element.23) | copy-start | bytes 294916

commit v2 on v1

v2 whole, which is shorter than its diff:
```python
import functools

import jax
import jax.numpy as jnp
from jax import lax
from jax.experimental import pallas as pl
from jax.experimental.pallas import tpu as pltpu
from jax.sharding import PartitionSpec as P

GRID = (4, 8, 2)
MESH = pl.DeviceIdType.MESH
F32 = jnp.float32
BF16 = jnp.bfloat16


def dot(left, right, dims):
    return lax.dot_general(left, right, (dims, ((), ())), preferred_element_type=F32)


def dot_nn(left, right):
    return dot(left, right, ((1,), (0,)))


def dot_nt(left, right):
    return dot(left, right, ((1,), (1,)))


def dot_tn(left, right):
    return dot(left, right, ((0,), (0,)))


class Place:
    def __init__(self, grid, reverse):
        self.nx, self.ny, _ = grid
        self.reverse = reverse
        ctx = lax.axis_index("ctx")
        self.head = lax.axis_index("head")
        self.core = lax.rem(ctx, 2)
        self.phys_y = lax.rem(ctx // 2, self.ny)
        self.phys_x = ctx // (2 * self.ny)
        self.y = self.ny - 1 - self.phys_y if reverse else self.phys_y
        self.x = self.nx - 1 - self.phys_x if reverse else self.phys_x
        self.order = 1 - self.core if reverse else self.core

    def device(self, x, y, core):
        return ((x * self.ny + y) * 2 + core, self.head)

    def partner(self):
        return self.device(self.phys_x, self.phys_y, 1 - self.core)

    def along_y(self, y):
        return self.device(self.phys_x, self.ny - 1 - y if self.reverse else y, self.core)

    def along_x(self, x):
        return self.device(self.nx - 1 - x if self.reverse else x, self.phys_y, self.core)


class Scan:
    def __init__(self, way, place, rate, lengths, refs, pending):
        self.way, self.place, self.rate, self.lengths = way, place, rate, lengths
        (self.loc, self.pair, self.csend, self.a1, self.tx, self.psend, self.a2, self.fsend, self.st) = refs[:9]
        (self.c_s, self.c_r, self.a1_s, self.a1_r, self.x_s, self.x_r, self.a2_s, self.a2_r, self.f_s, self.f_r) = refs[9:]
        self.pending = pending
        self.heads = self.loc.shape[2]
        self.rows = self.csend.shape[4]
        self.half = self.fsend.shape[3]
        self.name = ("fwd", "bwd")[way]

    def decay(self, h, tokens):
        return jnp.exp(jnp.full((1, 128), -self.rate[h], F32) * tokens)

    def copy(self, src, dst, send, recv, device):
        return pltpu.make_async_remote_copy(
            src_ref=src, dst_ref=dst, send_sem=send, recv_sem=recv, device_id=device, device_id_type=MESH
        )

    def start(self, copy):
        copy.start()
        self.pending.append(copy)

    def half_of(self, core):
        return pl.ds(pl.multiple_of(core * self.half, self.half), self.half)

    def pair_copy(self, s):
        w, p = self.way, self.place
        src = self.loc.at[w, s, :, self.half_of(1 - p.core), :]
        return self.copy(src, self.pair.at[w, s], self.c_s.at[w, s], self.c_r.at[w, s], p.partner())

    def start_pair(self, s):
        self.start(self.pair_copy(s))

    def first_second(self, s, h):
        own = self.loc[self.way, s, h, self.half_of(self.place.core), :]
        other = self.pair[self.way, s, h]
        leads = self.place.order == 0
        return jnp.where(leads, own, other), jnp.where(leads, other, own)

    def send_along_y(self, src, dst, send, recv, s):
        w, p = self.way, self.place
        for k in far_first(p.ny):
            to = lax.rem(p.y + k, p.ny)
            self.start(self.copy(src.at[w, s, to], dst.at[w, s, p.y], send.at[w, s, k], recv.at[w, s, p.y], p.along_y(to)))

    def wait_along(self, buf, sem, here, n, s, device):
        w = self.way
        for k in range(1, n):
            at = lax.rem(here + k, n)
            landed = buf.at[w, s, at]
            self.copy(landed, landed, sem.at[w, s, at], sem.at[w, s, at], device(at)).wait_recv()

    def chip(self, s):
        w, p = self.way, self.place
        with jax.named_scope(f"{self.name}_pair{s}"):
            self.pair_copy(s).wait_recv()
        for h in range(self.heads):
            first, second = self.first_second(s, h)
            both = self.decay(h, float(self.lengths[s])) * first + second
            for j in range(p.ny):
                self.csend[w, s, j, h] = both[j * self.rows : (j + 1) * self.rows]
        self.a1[w, s, p.y] = self.csend[w, s, p.y]
        self.send_along_y(self.csend, self.a1, self.a1_s, self.a1_r, s)

    def column(self, s):
        w, p = self.way, self.place
        with jax.named_scope(f"{self.name}_gather{s}"):
            self.wait_along(self.a1, self.a1_r, p.y, p.ny, s, p.along_y)
        for h in range(self.heads):
            step = self.decay(h, 2.0 * self.lengths[s])
            total = self.a1[w, s, 0, h]
            for j in range(1, p.ny):
                total = step * total + self.a1[w, s, j, h]
            self.tx[w, s, p.x, h] = total
        for k in far_first(p.nx):
            to = lax.rem(p.x + k, p.nx)
            mine = self.tx.at[w, s, p.x]
            self.start(self.copy(mine, mine, self.x_s.at[w, s, k], self.x_r.at[w, s, p.x], p.along_x(to)))

    def columns(self, s):
        w, p = self.way, self.place
        with jax.named_scope(f"{self.name}_x{s}"):
            self.wait_along(self.tx, self.x_r, p.x, p.nx, s, p.along_x)
        bases, totals = [], []
        for h in range(self.heads):
            step = self.decay(h, 2.0 * self.lengths[s] * p.ny)
            run = self.tx[w, s, 0, h]
            base = jnp.zeros_like(run)
            for j in range(1, p.nx):
                base = jnp.where(p.x == j, run, base)
                run = step * run + self.tx[w, s, j, h]
            bases.append(base)
            totals.append(run)
        return bases, totals

    def spread(self, s, bases, given):
        w, p = self.way, self.place
        for h in range(self.heads):
            step = self.decay(h, 2.0 * self.lengths[s])
            entry = bases[h]
            if given is not None:
                before = (p.x * (2 * p.ny * self.lengths[s])).astype(F32)
                entry = entry + self.decay(h, before) * given[h]
            for j in range(p.ny):
                self.psend[w, s, j, h] = entry
                if j < p.ny - 1:
                    entry = step * entry + self.a1[w, s, j, h]
        self.a2[w, s, p.y] = self.psend[w, s, p.y]
        self.send_along_y(self.psend, self.a2, self.a2_s, self.a2_r, s)

    def final_copy(self, s):
        w, p = self.way, self.place
        dst = self.st.at[w, s, :, self.half_of(p.core), :]
        return self.copy(self.fsend.at[w, s], dst, self.f_s.at[w, s], self.f_r.at[w, s], p.partner())

    def finish(self, s):
        w, p = self.way, self.place
        with jax.named_scope(f"{self.name}_spread{s}"):
            self.wait_along(self.a2, self.a2_r, p.y, p.ny, s, p.along_y)
        leads = p.order == 0
        for h in range(self.heads):
            entry = jnp.concatenate([self.a2[w, s, j, h] for j in range(p.ny)], axis=0)
            first, _ = self.first_second(s, h)
            after = self.decay(h, float(self.lengths[s])) * entry + first
            self.st[w, s, h, self.half_of(p.core), :] = jnp.where(leads, entry, after)
            self.fsend[w, s, h] = jnp.where(leads, after, entry)
        self.start(self.final_copy(s))

    def ready(self, s):
        w, p = self.way, self.place
        landed = self.st.at[w, s, :, self.half_of(1 - p.core), :]
        with jax.named_scope(f"{self.name}_last{s}"):
            self.copy(landed, landed, self.f_r.at[w, s], self.f_r.at[w, s], p.partner()).wait_recv()


def far_first(n):
    return sorted(range(1, n), key=lambda k: -min(k, n - k))


def column_of(row):
    return jnp.broadcast_to(row, (128, 128)).T


def kernel(
    grid, nz, *refs
):
    places = refs[:10]
    py, ry, pdq, pdk, pdv, rdq, rdk, rdv = refs[10:18]
    held = refs[18:28]
    rate, gain, pq, pk, pv, pc, rq, rk, rv, rc = held
    loc, pair, csend, a1, tx, psend, a2, fsend, st, stat, pmix, rmix, pout, rout, pgrad, rgrad, dk_p, dv_p, dk_r, dv_r = refs[28:48]
    in_s, c_s, c_r, a1_s, a1_r, x_s, x_r, a2_s, a2_r, f_s, f_r, z_s, z_r = refs[48:]
    loads = {id(dst): pltpu.make_async_copy(src, dst, in_s.at[i]) for i, (src, dst) in enumerate(zip(places, held))}
    for ref in (rate, pk, pv, rk, rv, gain, pq, rq, pc, rc):
        loads[id(ref)].start()

    def arrive(*wanted):
        for ref in wanted:
            loads[id(ref)].wait()

    heads, tokens, width = pq.shape
    count = rq.shape[2]
    features = float(heads * nz * width)
    ahead, back = Place(grid, False), Place(grid, True)
    ctx, z = lax.axis_index("ctx"), ahead.head

    barrier = pltpu.get_barrier_semaphore()
    peers = [ahead.partner()]
    peers += [ahead.along_y(lax.rem(ahead.y + k, grid[1])) for k in range(1, grid[1])]
    peers += [ahead.along_x(lax.rem(ahead.x + k, grid[0])) for k in range(1, grid[0])]
    peers += [(ctx, lax.rem(z + k, nz)) for k in range(1, nz)]
    for peer in peers:
        pl.semaphore_signal(barrier, inc=1, device_id=peer, device_id_type=MESH)

    pending = []
    refs = (loc, pair, csend, a1, tx, psend, a2, fsend, st, c_s, c_r, a1_s, a1_r, x_s, x_r, a2_s, a2_r, f_s, f_r)
    lengths = (tokens, count, count)
    fwd = Scan(0, ahead, rate, lengths, refs, pending)
    bwd = Scan(1, back, rate, lengths, refs, pending)

    row = lax.broadcasted_iota(jnp.int32, (128, 128), 0)
    col = lax.broadcasted_iota(jnp.int32, (128, 128), 1)
    lag = (row - col).astype(F32)
    causal = row >= col
    apart = (row // count) != (col // count)
    place_p = row.astype(F32)
    place_r = lax.rem(row, count).astype(F32)

    def power(h, steps):
        return jnp.exp(jnp.full((128, 128), -rate[h], F32) * steps)

    def pairs(ref, h):
        return jnp.concatenate([ref[0, h], ref[1, h]], axis=0)

    def masks(h):
        mask = jnp.where(causal, power(h, jnp.maximum(lag, 0.0)), 0.0)
        return mask, jnp.where(apart, 0.0, mask)

    def fwd_states(s):
        for h in range(heads):
            if s == 0:
                keys = (pk[h].astype(F32) * power(h, tokens - 1.0 - place_p)).astype(BF16)
                loc[0, 0, h] = dot_tn(keys, pv[h])
            else:
                keys = (rk[s - 1, h].astype(F32) * power(h, count - 1.0 - place_p)[:count]).astype(BF16)
                loc[0, s, h] = dot_tn(keys, rv[s - 1, h])

    with jax.named_scope("local_p"):
        arrive(rate, pk, pv)
        fwd_states(0)
    with jax.named_scope("entry"):
        pl.semaphore_wait(barrier, len(peers))
    fwd.start_pair(0)
    with jax.named_scope("local_r"):
        arrive(rk, rv)
        fwd_states(1)
        fwd.start_pair(1)
        fwd_states(2)
        fwd.start_pair(2)
    for s in range(3):
        fwd.chip(s)

    with jax.named_scope("intra"):
        arrive(pq, rq)
        for h in range(heads):
            mask_p, mask_r = masks(h)
            pmix[h] = (dot_nt(pq[h], pk[h]) * mask_p).astype(BF16)
            rmix[h] = (dot_nt(pairs(rq, h), pairs(rk, h)) * mask_r).astype(BF16)
            pout[h] = dot_nn(pmix[h], pv[h])
            rout[h] = dot_nn(rmix[h], pairs(rv, h))

    arrive(gain, pc, rc)
    fwd.column(0)
    fwd.column(1)
    bases, final = fwd.columns(0)
    fwd.spread(0, bases, None)
    fwd.column(2)
    for s in (1, 2):
        bases, _ = fwd.columns(s)
        fwd.spread(s, bases, final)

    def outputs(s):
        fwd.ready(s)
        rows = tokens if s == 0 else count
        part = slice(0, rows) if s == 0 else slice((s - 1) * count, s * count)
        squares, inner = jnp.zeros((rows, 128), F32), jnp.zeros((rows, 128), F32)
        for h in range(heads):
            buf = pout if s == 0 else rout
            queries, cot = (pq[h], pc[h]) if s == 0 else (rq[s - 1, h], rc[s - 1, h])
            across = dot_nn(queries, st[0, s, h].astype(BF16))
            out = buf[h, part, :] + power(h, place_p + 1.0)[:rows] * across
            buf[h, part, :] = out
            squares += out * out
            inner += gain[h : h + 1] * cot.astype(F32) * out
        both = [squares, inner] if s == 0 else [jnp.concatenate([squares, inner], axis=0)]
        lines = [jnp.sum(a.T, axis=0, keepdims=True) for a in both]
        stat[s, z] = jnp.concatenate(lines + [jnp.zeros((8 - len(lines), 128), F32)], axis=0)
        for k in far_first(nz):
            to = (ctx, lax.rem(z + k, nz))
            fwd.start(fwd.copy(stat.at[s, z], stat.at[s, z], z_s.at[s, k], z_r.at[s, z], to))

    def norms(s):
        with jax.named_scope(f"norm{s}"):
            for k in range(1, nz):
                at = lax.rem(z + k, nz)
                landed = stat.at[s, at]
                fwd.copy(landed, landed, z_r.at[s, at], z_r.at[s, at], (ctx, at)).wait_recv()
        total = stat[s, 0]
        for k in range(1, nz):
            total = total + stat[s, k]
        if s == 0:
            inv = lax.rsqrt(total[0:1] / features + 1e-05)
            return column_of(inv), column_of(total[1:2] * inv * inv * inv / features)
        both = column_of(total[0:1])
        inv = lax.rsqrt(both[:count] / features + 1e-05)
        return inv, both[count:] * inv * inv * inv / features

    def gradients(s):
        inv, coef = norms(s)
        rows = tokens if s == 0 else count
        part = slice(0, rows) if s == 0 else slice((s - 1) * count, s * count)
        for h in range(heads):
            out = (pout if s == 0 else rout)[h, part, :]
            queries, cot = (pq[h], pc[h]) if s == 0 else (rq[s - 1, h], rc[s - 1, h])
            grad = (gain[h : h + 1] * cot.astype(F32) * inv - out * coef).astype(BF16)
            if s == 0:
                pgrad[h] = grad
            else:
                rgrad[h, part, :] = grad
            queries = (queries.astype(F32) * power(h, place_p + 1.0)[:rows]).astype(BF16)
            loc[1, s, h] = dot_tn(queries, grad)
        bwd.start_pair(s)
        return inv

    def normed(s, inv):
        for h in range(heads):
            if s == 0:
                py[h] = (gain[h : h + 1] * pout[h] * inv).astype(BF16)
            else:
                ry[s - 1, h] = (gain[h : h + 1] * rout[h, (s - 1) * count : s * count, :] * inv).astype(BF16)

    fwd.finish(0)
    fwd.finish(1)
    outputs(0)
    fwd.finish(2)
    outputs(1)
    outputs(2)
    inv_p = gradients(0)
    inv_0 = gradients(1)
    bwd.chip(0)
    inv_1 = gradients(2)
    bwd.chip(1)
    bwd.chip(2)

    with jax.named_scope("inner"):
        for s, inv in enumerate((inv_p, inv_0, inv_1)):
            normed(s, inv)
        for h in range(heads):
            mask_p, mask_r = masks(h)
            grad = pgrad[h]
            dmix = (dot_nt(grad, pv[h]) * mask_p).astype(BF16)
            across = dot_nt(grad, st[0, 0, h].astype(BF16))
            pdq[h] = (dot_nn(dmix, pk[h]) + power(h, place_p + 1.0) * across).astype(BF16)
            dk_p[h] = dot_tn(dmix, pq[h])
            dv_p[h] = dot_tn(pmix[h], grad)
            grad = rgrad[h]
            dmix = (dot_nt(grad, pairs(rv, h)) * mask_r).astype(BF16)
            across = [dot_nt(grad[r * count : (r + 1) * count], st[0, 1 + r, h].astype(BF16)) for r in range(2)]
            queries = dot_nn(dmix, pairs(rk, h)) + power(h, place_r + 1.0) * jnp.concatenate(across, axis=0)
            dk_r[h] = dot_tn(dmix, pairs(rq, h))
            dv_r[h] = dot_tn(rmix[h], grad)
            for r in range(2):
                rdq[r, h] = queries[r * count : (r + 1) * count].astype(BF16)

    bwd.column(0)
    bwd.column(1)
    bwd.column(2)
    given = [0.0] * heads
    for s in (1, 2):
        bases, totals = bwd.columns(s)
        bwd.spread(s, bases, None)
        given = [a + b for a, b in zip(given, totals)]
    bases, _ = bwd.columns(0)
    bwd.spread(0, bases, given)

    def responses(r):
        bwd.ready(1 + r)
        part = slice(r * count, (r + 1) * count)
        for h in range(heads):
            later = st[1, 1 + r, h].astype(BF16)
            fade = power(h, count - 1.0 - place_p)[:count]
            rdk[r, h] = (dk_r[h, part, :] + fade * dot_nt(rv[r, h], later)).astype(BF16)
            rdv[r, h] = (dv_r[h, part, :] + fade * dot_nn(rk[r, h], later)).astype(BF16)

    bwd.finish(1)
    bwd.finish(2)
    responses(0)
    bwd.finish(0)
    responses(1)
    bwd.ready(0)
    with jax.named_scope("end"):
        for h in range(heads):
            later = st[1, 0, h].astype(BF16)
            fade = power(h, tokens - 1.0 - place_p)
            pdk[h] = (dk_p[h] + fade * dot_nt(pv[h], later)).astype(BF16)
            pdv[h] = (dv_p[h] + fade * dot_nn(pk[h], later)).astype(BF16)
        for copy in pending:
            copy.wait_send()


def hand_over(*refs):
    copies = [pltpu.make_async_copy(src, dst, refs[16].at[i]) for i, (src, dst) in enumerate(zip(refs[:8], refs[8:16]))]
    for copy in copies:
        copy.start()
    for copy in copies:
        copy.wait()


def shards(grid, nz, prompt_q, prompt_k, prompt_v, resp_q, resp_k, resp_v, decay_rate, norm_gain, prompt_cot, resp_cot):
    nx, ny, _ = grid
    tokens, heads, width = prompt_q.shape
    count = resp_q.shape[1]
    half, rows = width // 2, width // 2 // ny
    prompt = [jnp.transpose(a, (1, 0, 2)) for a in (prompt_q, prompt_k, prompt_v, prompt_cot)]
    resp = [jnp.transpose(a, (0, 2, 1, 3)) for a in (resp_q, resp_k, resp_v, resp_cot)]
    flat = pltpu.VMEM((heads, tokens, width), BF16)
    duo = pltpu.VMEM((2, heads, count, width), BF16)
    vmem, hbm = pl.BlockSpec(memory_space=pltpu.VMEM), pl.BlockSpec(memory_space=pltpu.HBM)
    block = (heads, tokens, width)
    scratch = [pltpu.SMEM((heads,), F32), pltpu.VMEM((heads, width), F32)]
    scratch += [pltpu.VMEM(block, BF16)] * 4 + [pltpu.VMEM((2, heads, count, width), BF16)] * 4
    scratch += [
        pltpu.VMEM((2, 3, heads, width, width), F32),
        pltpu.VMEM((2, 3, heads, half, width), F32),
        pltpu.VMEM((2, 3, ny, heads, rows, width), F32),
        pltpu.VMEM((2, 3, ny, heads, rows, width), F32),
        pltpu.VMEM((2, 3, nx, heads, rows, width), F32),
        pltpu.VMEM((2, 3, ny, heads, rows, width), F32),
        pltpu.VMEM((2, 3, ny, heads, rows, width), F32),
        pltpu.VMEM((2, 3, heads, half, width), F32),
        pltpu.VMEM((2, 3, heads, width, width), F32),
        pltpu.VMEM((3, nz, 8, width), F32),
        pltpu.VMEM(block, BF16),
        pltpu.VMEM(block, BF16),
        pltpu.VMEM(block, F32),
        pltpu.VMEM(block, F32),
        pltpu.VMEM(block, BF16),
        pltpu.VMEM(block, BF16),
        pltpu.VMEM(block, F32),
        pltpu.VMEM(block, F32),
        pltpu.VMEM(block, F32),
        pltpu.VMEM(block, F32),
    ]
    dma = pltpu.SemaphoreType.DMA
    scratch += [dma((10,))] + [dma((2, 3))] * 2 + [dma((2, 3, ny))] * 2 + [dma((2, 3, nx))] * 2
    scratch += [dma((2, 3, ny))] * 2 + [dma((2, 3))] * 2 + [dma((3, nz))] * 2
    out = pl.pallas_call(
        functools.partial(kernel, grid, nz),
        out_shape=(flat, duo, flat, flat, flat, duo, duo, duo),
        in_specs=[hbm] * 10,
        out_specs=(vmem,) * 8,
        scratch_shapes=scratch,
        compiler_params=pltpu.CompilerParams(collective_id=0, has_side_effects=True, vmem_limit_bytes=40 << 20),
    )(*(pltpu.with_memory_space_constraint(a, pltpu.HBM) for a in (decay_rate, norm_gain, *prompt, *resp)))
    out = pl.pallas_call(
        hand_over,
        out_shape=tuple(jax.ShapeDtypeStruct(a.shape, a.dtype) for a in out),
        in_specs=[vmem] * 8,
        out_specs=(hbm,) * 8,
        scratch_shapes=[dma((8,))],
        compiler_params=pltpu.CompilerParams(vmem_limit_bytes=8 << 20),
    )(*out)
    return tuple(
        jnp.transpose(a, (1, 0, 2)) if a.ndim == 3 else jnp.transpose(a, (0, 2, 1, 3)) for a in out
    )


def solution(mesh):
    flat, duo = P("ctx", "head", None), P(None, "ctx", "head", None)
    return jax.shard_map(
        functools.partial(shards, GRID, mesh.shape["head"]),
        mesh=mesh,
        in_specs=(flat, flat, flat, duo, duo, duo, P("head"), P("head", None), flat, duo),
        out_specs=(flat, duo, flat, flat, flat, duo, duo, duo),
        check_vma=False,
    )
```

time: 79.8 us -> 70.2 us (0.88)
  local copies, waits for them, and re-layouts: 7.79 us -> 0 us
  Pallas kernels: 71 us -> 69.4 us
    unnamed x22 -> x0, local copies, waits for them, and re-layouts: 7.79 us -> none
    pallas_call x1, Pallas kernels: 71 us -> 68.5 us  [shards(): pl.pallas_call(functools.partial(kernel, grid, nz), out_shape=(flat, duo,...]
    pallas_call x0 -> x1, Pallas kernels: none -> 0.94 us  [shards(): pl.pallas_call(hand_over, out_shape=tuple((jax.ShapeDtypeStruct(a.shape,...]
where the time goes in v2:
time: 70.2 us; the launch traced here: 70.1 us
  Pallas kernels  69.4 us (99%)
    pallas_call x1, Pallas kernels, shards(): pl.pallas_call(functools.partial(kernel, grid, nz), out_shape=(flat, duo,...  68.5 us

profile of v2, /device:TPU:1, one launch (start us, length us, event | category | flops | bytes accessed | tf_op | source)
XLA Modules:
  0.0 70.1 jit_solution(9945897353351738438)
XLA Ops:
  0.6 68.5 %shard_map.161 = (bf16[3,128,128]{2,1,0:T(8,128)(2,1)S(1)}, bf16[2,3,64,128]{3,2,1,0:T(8,128)(2,1)S(1)}, bf16[3,128,128]{2,1,0:T(8,128)(2,1)S(1)}, bf16[3,128,12...) custom-call(f32[3]{0:T(128)} %refs_0_.1, ...), custom_call_target="tpu_custom_call" | custom-call | tf_op jit(solution)/shard_map/pallas_call | solution.py:475
  69.1 0.9 %shard_map.162 = (bf16[3,128,128]{2,1,0:T(8,128)(2,1)}, bf16[2,3,64,128]{3,2,1,0:T(8,128)(2,1)}, bf16[3,128,128]{2,1,0:T(8,128)(2,1)}, bf16[3,128,128]{2,1,0:T(8...) custom-call(bf16[3,128,128]{2,1,0:T(8,128)(2,1)S(1)} %get-tuple-elem, ...), custom_call_target="tpu_custom_call" | custom-call | tf_op jit(solution)/shard_map/pallas_call | solution.py:483

commit v3 on v2

--- a/solution.py
+++ b/solution.py
@@ -56,11 +56,10 @@
 
 
 class Scan:
-    def __init__(self, way, place, rate, lengths, refs, pending):
+    def __init__(self, way, place, rate, lengths, refs):
         self.way, self.place, self.rate, self.lengths = way, place, rate, lengths
         (self.loc, self.pair, self.csend, self.a1, self.tx, self.psend, self.a2, self.fsend, self.st) = refs[:9]
         (self.c_s, self.c_r, self.a1_s, self.a1_r, self.x_s, self.x_r, self.a2_s, self.a2_r, self.f_s, self.f_r) = refs[9:]
-        self.pending = pending
         self.heads = self.loc.shape[2]
         self.rows = self.csend.shape[4]
         self.half = self.fsend.shape[3]
@@ -74,20 +73,16 @@
             src_ref=src, dst_ref=dst, send_sem=send, recv_sem=recv, device_id=device, device_id_type=MESH
         )
 
-    def start(self, copy):
-        copy.start()
-        self.pending.append(copy)
-
     def half_of(self, core):
         return pl.ds(pl.multiple_of(core * self.half, self.half), self.half)
 
     def pair_copy(self, s):
         w, p = self.way, self.place
         src = self.loc.at[w, s, :, self.half_of(1 - p.core), :]
-        return self.copy(src, self.pair.at[w, s], self.c_s.at[w, s], self.c_r.at[w, s], p.partner())
+        return self.copy(src, self.pair.at[w, s], self.c_s, self.c_r.at[w, s], p.partner())
 
     def start_pair(self, s):
-        self.start(self.pair_copy(s))
+        self.pair_copy(s).start()
 
     def first_second(self, s, h):
         own = self.loc[self.way, s, h, self.half_of(self.place.core), :]
@@ -99,14 +94,11 @@
         w, p = self.way, self.place
         for k in far_first(p.ny):
             to = lax.rem(p.y + k, p.ny)
-            self.start(self.copy(src.at[w, s, to], dst.at[w, s, p.y], send.at[w, s, k], recv.at[w, s, p.y], p.along_y(to)))
-
-    def wait_along(self, buf, sem, here, n, s, device):
-        w = self.way
-        for k in range(1, n):
-            at = lax.rem(here + k, n)
-            landed = buf.at[w, s, at]
-            self.copy(landed, landed, sem.at[w, s, at], sem.at[w, s, at], device(at)).wait_recv()
+            self.copy(src.at[w, s, to], dst.at[w, s, p.y], send, recv.at[w, s], p.along_y(to)).start()
+
+    def wait_all(self, buf, sem, s):
+        others = buf.at[self.way, s, pl.ds(0, buf.shape[2] - 1)]
+        self.copy(others, others, sem.at[self.way, s], sem.at[self.way, s], self.place.partner()).wait_recv()
 
     def chip(self, s):
         w, p = self.way, self.place
@@ -123,7 +115,7 @@
     def column(self, s):
         w, p = self.way, self.place
         with jax.named_scope(f"{self.name}_gather{s}"):
-            self.wait_along(self.a1, self.a1_r, p.y, p.ny, s, p.along_y)
+            self.wait_all(self.a1, self.a1_r, s)
         for h in range(self.heads):
             step = self.decay(h, 2.0 * self.lengths[s])
             total = self.a1[w, s, 0, h]
@@ -133,12 +125,12 @@
         for k in far_first(p.nx):
             to = lax.rem(p.x + k, p.nx)
             mine = self.tx.at[w, s, p.x]
-            self.start(self.copy(mine, mine, self.x_s.at[w, s, k], self.x_r.at[w, s, p.x], p.along_x(to)))
+            self.copy(mine, mine, self.x_s, self.x_r.at[w, s], p.along_x(to)).start()
 
     def columns(self, s):
         w, p = self.way, self.place
         with jax.named_scope(f"{self.name}_x{s}"):
-            self.wait_along(self.tx, self.x_r, p.x, p.nx, s, p.along_x)
+            self.wait_all(self.tx, self.x_r, s)
         bases, totals = [], []
         for h in range(self.heads):
             step = self.decay(h, 2.0 * self.lengths[s] * p.ny)
@@ -169,12 +161,12 @@
     def final_copy(self, s):
         w, p = self.way, self.place
         dst = self.st.at[w, s, :, self.half_of(p.core), :]
-        return self.copy(self.fsend.at[w, s], dst, self.f_s.at[w, s], self.f_r.at[w, s], p.partner())
+        return self.copy(self.fsend.at[w, s], dst, self.f_s, self.f_r.at[w, s], p.partner())
 
     def finish(self, s):
         w, p = self.way, self.place
         with jax.named_scope(f"{self.name}_spread{s}"):
-            self.wait_along(self.a2, self.a2_r, p.y, p.ny, s, p.along_y)
+            self.wait_all(self.a2, self.a2_r, s)
         leads = p.order == 0
         for h in range(self.heads):
             entry = jnp.concatenate([self.a2[w, s, j, h] for j in range(p.ny)], axis=0)
@@ -182,7 +174,7 @@
             after = self.decay(h, float(self.lengths[s])) * entry + first
             self.st[w, s, h, self.half_of(p.core), :] = jnp.where(leads, entry, after)
             self.fsend[w, s, h] = jnp.where(leads, after, entry)
-        self.start(self.final_copy(s))
+        self.final_copy(s).start()
 
     def ready(self, s):
         w, p = self.way, self.place
@@ -193,6 +185,14 @@
 
 def far_first(n):
     return sorted(range(1, n), key=lambda k: -min(k, n - k))
+
+
+def reaching(n):
+    strides, reach = [], 1
+    while reach < n // 2:
+        strides.append(min(reach, n // 2 - reach))
+        reach += strides[-1]
+    return strides
 
 
 def column_of(row):
@@ -207,7 +207,7 @@
     held = refs[18:28]
     rate, gain, pq, pk, pv, pc, rq, rk, rv, rc = held
     loc, pair, csend, a1, tx, psend, a2, fsend, st, stat, pmix, rmix, pout, rout, pgrad, rgrad, dk_p, dv_p, dk_r, dv_r = refs[28:48]
-    in_s, c_s, c_r, a1_s, a1_r, x_s, x_r, a2_s, a2_r, f_s, f_r, z_s, z_r = refs[48:]
+    in_s, c_s, c_r, a1_s, a1_r, x_s, x_r, a2_s, a2_r, f_s, f_r, z_s, z_r, told = refs[48:]
     loads = {id(dst): pltpu.make_async_copy(src, dst, in_s.at[i]) for i, (src, dst) in enumerate(zip(places, held))}
     for ref in (rate, pk, pv, rk, rv, gain, pq, rq, pc, rc):
         loads[id(ref)].start()
@@ -226,15 +226,14 @@
     peers = [ahead.partner()]
     peers += [ahead.along_y(lax.rem(ahead.y + k, grid[1])) for k in range(1, grid[1])]
     peers += [ahead.along_x(lax.rem(ahead.x + k, grid[0])) for k in range(1, grid[0])]
-    peers += [(ctx, lax.rem(z + k, nz)) for k in range(1, nz)]
+    peers += [(ctx, lax.rem(z + 1, nz)), (ctx, lax.rem(z + nz - 1, nz))]
     for peer in peers:
         pl.semaphore_signal(barrier, inc=1, device_id=peer, device_id_type=MESH)
 
-    pending = []
     refs = (loc, pair, csend, a1, tx, psend, a2, fsend, st, c_s, c_r, a1_s, a1_r, x_s, x_r, a2_s, a2_r, f_s, f_r)
     lengths = (tokens, count, count)
-    fwd = Scan(0, ahead, rate, lengths, refs, pending)
-    bwd = Scan(1, back, rate, lengths, refs, pending)
+    fwd = Scan(0, ahead, rate, lengths, refs)
+    bwd = Scan(1, back, rate, lengths, refs)
 
     row = lax.broadcasted_iota(jnp.int32, (128, 128), 0)
     col = lax.broadcasted_iota(jnp.int32, (128, 128), 1)
@@ -254,6 +253,20 @@
         mask = jnp.where(causal, power(h, jnp.maximum(lag, 0.0)), 0.0)
         return mask, jnp.where(apart, 0.0, mask)
 
+    strides = reaching(nz)
+
+    def tell(i):
+        for side, stride in enumerate((strides[i], nz - strides[i])):
+            to = (ctx, lax.rem(z + stride, nz))
+            pl.semaphore_signal(told.at[i, side], inc=1, device_id=to, device_id_type=MESH)
+
+    def hear(i):
+        with jax.named_scope(f"hear{i}"):
+            for side in range(2):
+                pl.semaphore_wait(told.at[i, side], 1)
+        if i + 1 < len(strides):
+            tell(i + 1)
+
     def fwd_states(s):
         for h in range(heads):
             if s == 0:
@@ -269,6 +282,8 @@
     with jax.named_scope("entry"):
         pl.semaphore_wait(barrier, len(peers))
     fwd.start_pair(0)
+    if strides:
+        tell(0)
     with jax.named_scope("local_r"):
         arrive(rk, rv)
         fwd_states(1)
@@ -277,6 +292,8 @@
         fwd.start_pair(2)
     for s in range(3):
         fwd.chip(s)
+    if strides:
+        hear(0)
 
     with jax.named_scope("intra"):
         arrive(pq, rq)
@@ -288,7 +305,11 @@
             rout[h] = dot_nn(rmix[h], pairs(rv, h))
 
     arrive(gain, pc, rc)
+    if len(strides) > 1:
+        hear(1)
     fwd.column(0)
+    for i in range(2, len(strides)):
+        hear(i)
     fwd.column(1)
     bases, final = fwd.columns(0)
     fwd.spread(0, bases, None)
@@ -315,14 +336,12 @@
         stat[s, z] = jnp.concatenate(lines + [jnp.zeros((8 - len(lines), 128), F32)], axis=0)
         for k in far_first(nz):
             to = (ctx, lax.rem(z + k, nz))
-            fwd.start(fwd.copy(stat.at[s, z], stat.at[s, z], z_s.at[s, k], z_r.at[s, z], to))
+            fwd.copy(stat.at[s, z], stat.at[s, z], z_s, z_r.at[s], to).start()
 
     def norms(s):
         with jax.named_scope(f"norm{s}"):
-            for k in range(1, nz):
-                at = lax.rem(z + k, nz)
-                landed = stat.at[s, at]
-                fwd.copy(landed, landed, z_r.at[s, at], z_r.at[s, at], (ctx, at)).wait_recv()
+            others = stat.at[s, pl.ds(0, nz - 1)]
+            fwd.copy(others, others, z_r.at[s], z_r.at[s], ahead.partner()).wait_recv()
         total = stat[s, 0]
         for k in range(1, nz):
             total = total + stat[s, k]
@@ -357,21 +376,16 @@
             else:
                 ry[s - 1, h] = (gain[h : h + 1] * rout[h, (s - 1) * count : s * count, :] * inv).astype(BF16)
 
-    fwd.finish(0)
-    fwd.finish(1)
-    outputs(0)
-    fwd.finish(2)
-    outputs(1)
-    outputs(2)
-    inv_p = gradients(0)
-    inv_0 = gradients(1)
-    bwd.chip(0)
-    inv_1 = gradients(2)
-    bwd.chip(1)
-    bwd.chip(2)
+    for s in range(3):
+        fwd.finish(s)
+        outputs(s)
+    scales = []
+    for s in range(3):
+        scales.append(gradients(s))
+        bwd.chip(s)
 
     with jax.named_scope("inner"):
-        for s, inv in enumerate((inv_p, inv_0, inv_1)):
+        for s, inv in enumerate(scales):
             normed(s, inv)
         for h in range(heads):
             mask_p, mask_r = masks(h)
@@ -411,8 +425,8 @@
             rdv[r, h] = (dv_r[h, part, :] + fade * dot_nn(rk[r, h], later)).astype(BF16)
 
     bwd.finish(1)
+    responses(0)
     bwd.finish(2)
-    responses(0)
     bwd.finish(0)
     responses(1)
     bwd.ready(0)
@@ -422,8 +436,13 @@
             fade = power(h, tokens - 1.0 - place_p)
             pdk[h] = (dk_p[h] + fade * dot_nt(pv[h], later)).astype(BF16)
             pdv[h] = (dv_p[h] + fade * dot_nn(pk[h], later)).astype(BF16)
-        for copy in pending:
-            copy.wait_send()
+        ny, nx = grid[1], grid[0]
+        sent = (
+            (pair, c_s), (csend.at[:, :, pl.ds(0, ny - 1)], a1_s), (tx.at[:, :, pl.ds(0, nx - 1)], x_s),
+            (psend.at[:, :, pl.ds(0, ny - 1)], a2_s), (fsend, f_s), (stat.at[:, pl.ds(0, nz - 1)], z_s),
+        )
+        for part, sem in sent:
+            fwd.copy(part, part, sem, sem, ahead.partner()).wait_send()
 
 
 def hand_over(*refs):
@@ -470,8 +489,8 @@
         pltpu.VMEM(block, F32),
     ]
     dma = pltpu.SemaphoreType.DMA
-    scratch += [dma((10,))] + [dma((2, 3))] * 2 + [dma((2, 3, ny))] * 2 + [dma((2, 3, nx))] * 2
-    scratch += [dma((2, 3, ny))] * 2 + [dma((2, 3))] * 2 + [dma((3, nz))] * 2
+    scratch += [dma((10,))] + [dma, dma((2, 3))] * 5 + [dma, dma((3,))]
+    scratch += [pltpu.SemaphoreType.REGULAR((max(1, len(reaching(nz))), 2))]
     out = pl.pallas_call(
         functools.partial(kernel, grid, nz),
         out_shape=(flat, duo, flat, flat, flat, duo, duo, duo),

time: 70.2 us -> 64.1 us (0.913)
  Pallas kernels: 69.4 us -> 63.3 us
    pallas_call x1, Pallas kernels: 68.5 us -> 62.4 us  [shards(): pl.pallas_call(functools.partial(kernel, grid, nz), out_shape=(flat, duo,...]
where the time goes in v3:
time: 64.1 us; the launch traced here: 64 us
  Pallas kernels  63.3 us (99%)
    pallas_call x1, Pallas kernels, shards(): pl.pallas_call(functools.partial(kernel, grid, nz), out_shape=(flat, duo,...  62.4 us

profile of v3, /device:TPU:1, one launch (start us, length us, event | category | flops | bytes accessed | tf_op | source)
XLA Modules:
  0.0 64.0 jit_solution(5107963670478488342)
XLA Ops:
  0.6 62.4 %shard_map.161 = (bf16[3,128,128]{2,1,0:T(8,128)(2,1)S(1)}, bf16[2,3,64,128]{3,2,1,0:T(8,128)(2,1)S(1)}, bf16[3,128,128]{2,1,0:T(8,128)(2,1)S(1)}, bf16[3,128,12...) custom-call(f32[3]{0:T(128)} %refs_0_.1, ...), custom_call_target="tpu_custom_call" | custom-call | tf_op jit(solution)/shard_map/pallas_call | solution.py:494
  63.0 0.9 %shard_map.162 = (bf16[3,128,128]{2,1,0:T(8,128)(2,1)}, bf16[2,3,64,128]{3,2,1,0:T(8,128)(2,1)}, bf16[3,128,128]{2,1,0:T(8,128)(2,1)}, bf16[3,128,128]{2,1,0:T(8...) custom-call(bf16[3,128,128]{2,1,0:T(8,128)(2,1)S(1)} %get-tuple-elem, ...), custom_call_target="tpu_custom_call" | custom-call | tf_op jit(solution)/shard_map/pallas_call | solution.py:502

commit v4 on v3

--- a/solution.py
+++ b/solution.py
@@ -206,12 +206,8 @@
     py, ry, pdq, pdk, pdv, rdq, rdk, rdv = refs[10:18]
     held = refs[18:28]
     rate, gain, pq, pk, pv, pc, rq, rk, rv, rc = held
-    loc, pair, csend, a1, tx, psend, a2, fsend, st, stat, pmix, rmix, pout, rout, pgrad, rgrad, dk_p, dv_p, dk_r, dv_r = refs[28:48]
-    in_s, c_s, c_r, a1_s, a1_r, x_s, x_r, a2_s, a2_r, f_s, f_r, z_s, z_r, told = refs[48:]
-    loads = {id(dst): pltpu.make_async_copy(src, dst, in_s.at[i]) for i, (src, dst) in enumerate(zip(places, held))}
-    for ref in (rate, pk, pv, rk, rv, gain, pq, rq, pc, rc):
-        loads[id(ref)].start()
-
+    loc, pair, csend, a1, tx, psend, a2, fsend, st, stat, pmix, rmix, pout, rout, pgrad, rgrad, dk_p, dv_p, dk_r, dv_r, pfade, rfade = refs[28:50]
+    in_s, c_s, c_r, a1_s, a1_r, x_s, x_r, a2_s, a2_r, f_s, f_r, z_s, z_r, told = refs[50:]
     def arrive(*wanted):
         for ref in wanted:
             loads[id(ref)].wait()
@@ -223,12 +219,15 @@
     ctx, z = lax.axis_index("ctx"), ahead.head
 
     barrier = pltpu.get_barrier_semaphore()
-    peers = [ahead.partner()]
-    peers += [ahead.along_y(lax.rem(ahead.y + k, grid[1])) for k in range(1, grid[1])]
+    peers = [ahead.along_y(lax.rem(ahead.y + k, grid[1])) for k in far_first(grid[1])]
     peers += [ahead.along_x(lax.rem(ahead.x + k, grid[0])) for k in range(1, grid[0])]
-    peers += [(ctx, lax.rem(z + 1, nz)), (ctx, lax.rem(z + nz - 1, nz))]
+    peers += [ahead.partner(), (ctx, lax.rem(z + 1, nz)), (ctx, lax.rem(z + nz - 1, nz))]
     for peer in peers:
         pl.semaphore_signal(barrier, inc=1, device_id=peer, device_id_type=MESH)
+
+    loads = {id(dst): pltpu.make_async_copy(src, dst, in_s.at[i]) for i, (src, dst) in enumerate(zip(places, held))}
+    for ref in (rate, pk, pv, rk, rv, gain, pq, rq, pc, rc):
+        loads[id(ref)].start()
 
     refs = (loc, pair, csend, a1, tx, psend, a2, fsend, st, c_s, c_r, a1_s, a1_r, x_s, x_r, a2_s, a2_r, f_s, f_r)
     lengths = (tokens, count, count)
@@ -303,6 +302,8 @@
             rmix[h] = (dot_nt(pairs(rq, h), pairs(rk, h)) * mask_r).astype(BF16)
             pout[h] = dot_nn(pmix[h], pv[h])
             rout[h] = dot_nn(rmix[h], pairs(rv, h))
+            pfade[h] = (pq[h].astype(F32) * power(h, place_p + 1.0)).astype(BF16)
+            rfade[h] = (pairs(rq, h).astype(F32) * power(h, place_r + 1.0)).astype(BF16)
 
     arrive(gain, pc, rc)
     if len(strides) > 1:
@@ -358,14 +359,13 @@
         part = slice(0, rows) if s == 0 else slice((s - 1) * count, s * count)
         for h in range(heads):
             out = (pout if s == 0 else rout)[h, part, :]
-            queries, cot = (pq[h], pc[h]) if s == 0 else (rq[s - 1, h], rc[s - 1, h])
+            cot = pc[h] if s == 0 else rc[s - 1, h]
             grad = (gain[h : h + 1] * cot.astype(F32) * inv - out * coef).astype(BF16)
             if s == 0:
                 pgrad[h] = grad
             else:
                 rgrad[h, part, :] = grad
-            queries = (queries.astype(F32) * power(h, place_p + 1.0)[:rows]).astype(BF16)
-            loc[1, s, h] = dot_tn(queries, grad)
+            loc[1, s, h] = dot_tn(pfade[h] if s == 0 else rfade[h, part, :], grad)
         bwd.start_pair(s)
         return inv
 
@@ -407,13 +407,12 @@
     bwd.column(0)
     bwd.column(1)
     bwd.column(2)
-    given = [0.0] * heads
-    for s in (1, 2):
-        bases, totals = bwd.columns(s)
-        bwd.spread(s, bases, None)
-        given = [a + b for a, b in zip(given, totals)]
+    bases_0, totals_0 = bwd.columns(1)
+    bwd.spread(1, bases_0, None)
+    bases_1, totals_1 = bwd.columns(2)
     bases, _ = bwd.columns(0)
-    bwd.spread(0, bases, given)
+    bwd.spread(0, bases, [a + b for a, b in zip(totals_0, totals_1)])
+    bwd.spread(2, bases_1, None)
 
     def responses(r):
         bwd.ready(1 + r)
@@ -424,11 +423,19 @@
             rdk[r, h] = (dk_r[h, part, :] + fade * dot_nt(rv[r, h], later)).astype(BF16)
             rdv[r, h] = (dv_r[h, part, :] + fade * dot_nn(rk[r, h], later)).astype(BF16)
 
+    ny, nx = grid[1], grid[0]
+
+    def sent(part, sem):
+        fwd.copy(part, part, sem, sem, ahead.partner()).wait_send()
+
+    sent(pair, c_s)
+    sent(csend.at[:, :, pl.ds(0, ny - 1)], a1_s)
+    sent(tx.at[:, :, pl.ds(0, nx - 1)], x_s)
+    sent(stat.at[:, pl.ds(0, nz - 1)], z_s)
     bwd.finish(1)
     responses(0)
+    bwd.finish(0)
     bwd.finish(2)
-    bwd.finish(0)
-    responses(1)
     bwd.ready(0)
     with jax.named_scope("end"):
         for h in range(heads):
@@ -436,13 +443,9 @@
             fade = power(h, tokens - 1.0 - place_p)
             pdk[h] = (dk_p[h] + fade * dot_nt(pv[h], later)).astype(BF16)
             pdv[h] = (dv_p[h] + fade * dot_nn(pk[h], later)).astype(BF16)
-        ny, nx = grid[1], grid[0]
-        sent = (
-            (pair, c_s), (csend.at[:, :, pl.ds(0, ny - 1)], a1_s), (tx.at[:, :, pl.ds(0, nx - 1)], x_s),
-            (psend.at[:, :, pl.ds(0, ny - 1)], a2_s), (fsend, f_s), (stat.at[:, pl.ds(0, nz - 1)], z_s),
-        )
-        for part, sem in sent:
-            fwd.copy(part, part, sem, sem, ahead.partner()).wait_send()
+    responses(1)
+    sent(psend.at[:, :, pl.ds(0, ny - 1)], a2_s)
+    sent(fsend, f_s)
 
 
 def hand_over(*refs):
@@ -488,6 +491,7 @@
         pltpu.VMEM(block, F32),
         pltpu.VMEM(block, F32),
     ]
+    scratch += [pltpu.VMEM(block, BF16)] * 2
     dma = pltpu.SemaphoreType.DMA
     scratch += [dma((10,))] + [dma, dma((2, 3))] * 5 + [dma, dma((3,))]
     scratch += [pltpu.SemaphoreType.REGULAR((max(1, len(reaching(nz))), 2))]

time: 64.1 us -> 63.7 us (level)
  no operation moved by 1% of the time
where the time goes in v4:
time: 63.7 us; the launch traced here: 63.6 us
  Pallas kernels  62.9 us (99%)
  between operations  0.64 us (1%)
    pallas_call x1, Pallas kernels, shards(): pl.pallas_call(functools.partial(kernel, grid, nz), out_shape=(flat, duo,...  62 us

profile of v4, /device:TPU:1, one launch (start us, length us, event | category | flops | bytes accessed | tf_op | source)
XLA Modules:
  0.0 63.6 jit_solution(2849061341133744033)
XLA Ops:
  0.6 62.0 %shard_map.161 = (bf16[3,128,128]{2,1,0:T(8,128)(2,1)S(1)}, bf16[2,3,64,128]{3,2,1,0:T(8,128)(2,1)S(1)}, bf16[3,128,128]{2,1,0:T(8,128)(2,1)S(1)}, bf16[3,128,12...) custom-call(f32[3]{0:T(128)} %refs_0_.1, ...), custom_call_target="tpu_custom_call" | custom-call | tf_op jit(solution)/shard_map/pallas_call | solution.py:498
  62.6 0.9 %shard_map.162 = (bf16[3,128,128]{2,1,0:T(8,128)(2,1)}, bf16[2,3,64,128]{3,2,1,0:T(8,128)(2,1)}, bf16[3,128,128]{2,1,0:T(8,128)(2,1)}, bf16[3,128,128]{2,1,0:T(8...) custom-call(bf16[3,128,128]{2,1,0:T(8,128)(2,1)S(1)} %get-tuple-elem, ...), custom_call_target="tpu_custom_call" | custom-call | tf_op jit(solution)/shard_map/pallas_call | solution.py:506

commit v5 on v4

--- a/solution.py
+++ b/solution.py
@@ -206,8 +206,8 @@
     py, ry, pdq, pdk, pdv, rdq, rdk, rdv = refs[10:18]
     held = refs[18:28]
     rate, gain, pq, pk, pv, pc, rq, rk, rv, rc = held
-    loc, pair, csend, a1, tx, psend, a2, fsend, st, stat, pmix, rmix, pout, rout, pgrad, rgrad, dk_p, dv_p, dk_r, dv_r, pfade, rfade = refs[28:50]
-    in_s, c_s, c_r, a1_s, a1_r, x_s, x_r, a2_s, a2_r, f_s, f_r, z_s, z_r, told = refs[50:]
+    loc, pair, csend, a1, tx, psend, a2, fsend, st, stat, pmix, rmix, pout, rout, pgrad, rgrad, dk_p, dv_p, dk_r, dv_r, pfade, rfade, pstep, rstep, pcot, rcot = refs[28:54]
+    in_s, c_s, c_r, a1_s, a1_r, x_s, x_r, a2_s, a2_r, f_s, f_r, z_s, z_r, told = refs[54:]
     def arrive(*wanted):
         for ref in wanted:
             loads[id(ref)].wait()
@@ -295,17 +295,20 @@
         hear(0)
 
     with jax.named_scope("intra"):
-        arrive(pq, rq)
+        arrive(pq, rq, gain, pc, rc)
         for h in range(heads):
             mask_p, mask_r = masks(h)
             pmix[h] = (dot_nt(pq[h], pk[h]) * mask_p).astype(BF16)
             rmix[h] = (dot_nt(pairs(rq, h), pairs(rk, h)) * mask_r).astype(BF16)
             pout[h] = dot_nn(pmix[h], pv[h])
             rout[h] = dot_nn(rmix[h], pairs(rv, h))
-            pfade[h] = (pq[h].astype(F32) * power(h, place_p + 1.0)).astype(BF16)
-            rfade[h] = (pairs(rq, h).astype(F32) * power(h, place_r + 1.0)).astype(BF16)
-
-    arrive(gain, pc, rc)
+            pstep[h] = power(h, place_p + 1.0)
+            rstep[h] = power(h, place_r + 1.0)
+            pfade[h] = (pq[h].astype(F32) * pstep[h]).astype(BF16)
+            rfade[h] = (pairs(rq, h).astype(F32) * rstep[h]).astype(BF16)
+            pcot[h] = gain[h : h + 1] * pc[h].astype(F32)
+            rcot[h] = gain[h : h + 1] * pairs(rc, h).astype(F32)
+
     if len(strides) > 1:
         hear(1)
     fwd.column(0)
@@ -326,12 +329,13 @@
         squares, inner = jnp.zeros((rows, 128), F32), jnp.zeros((rows, 128), F32)
         for h in range(heads):
             buf = pout if s == 0 else rout
-            queries, cot = (pq[h], pc[h]) if s == 0 else (rq[s - 1, h], rc[s - 1, h])
+            queries, cot = (pq[h], pcot[h]) if s == 0 else (rq[s - 1, h], rcot[h, part, :])
+            step = pstep[h] if s == 0 else rstep[h, part, :]
             across = dot_nn(queries, st[0, s, h].astype(BF16))
-            out = buf[h, part, :] + power(h, place_p + 1.0)[:rows] * across
+            out = buf[h, part, :] + step * across
             buf[h, part, :] = out
             squares += out * out
-            inner += gain[h : h + 1] * cot.astype(F32) * out
+            inner += cot * out
         both = [squares, inner] if s == 0 else [jnp.concatenate([squares, inner], axis=0)]
         lines = [jnp.sum(a.T, axis=0, keepdims=True) for a in both]
         stat[s, z] = jnp.concatenate(lines + [jnp.zeros((8 - len(lines), 128), F32)], axis=0)
@@ -359,8 +363,8 @@
         part = slice(0, rows) if s == 0 else slice((s - 1) * count, s * count)
         for h in range(heads):
             out = (pout if s == 0 else rout)[h, part, :]
-            cot = pc[h] if s == 0 else rc[s - 1, h]
-            grad = (gain[h : h + 1] * cot.astype(F32) * inv - out * coef).astype(BF16)
+            cot = pcot[h] if s == 0 else rcot[h, part, :]
+            grad = (cot * inv - out * coef).astype(BF16)
             if s == 0:
                 pgrad[h] = grad
             else:
@@ -392,13 +396,13 @@
             grad = pgrad[h]
             dmix = (dot_nt(grad, pv[h]) * mask_p).astype(BF16)
             across = dot_nt(grad, st[0, 0, h].astype(BF16))
-            pdq[h] = (dot_nn(dmix, pk[h]) + power(h, place_p + 1.0) * across).astype(BF16)
+            pdq[h] = (dot_nn(dmix, pk[h]) + pstep[h] * across).astype(BF16)
             dk_p[h] = dot_tn(dmix, pq[h])
             dv_p[h] = dot_tn(pmix[h], grad)
             grad = rgrad[h]
             dmix = (dot_nt(grad, pairs(rv, h)) * mask_r).astype(BF16)
             across = [dot_nt(grad[r * count : (r + 1) * count], st[0, 1 + r, h].astype(BF16)) for r in range(2)]
-            queries = dot_nn(dmix, pairs(rk, h)) + power(h, place_r + 1.0) * jnp.concatenate(across, axis=0)
+            queries = dot_nn(dmix, pairs(rk, h)) + rstep[h] * jnp.concatenate(across, axis=0)
             dk_r[h] = dot_tn(dmix, pairs(rq, h))
             dv_r[h] = dot_tn(rmix[h], grad)
             for r in range(2):
@@ -491,7 +495,7 @@
         pltpu.VMEM(block, F32),
         pltpu.VMEM(block, F32),
     ]
-    scratch += [pltpu.VMEM(block, BF16)] * 2
+    scratch += [pltpu.VMEM(block, BF16)] * 2 + [pltpu.VMEM(block, F32)] * 4
     dma = pltpu.SemaphoreType.DMA
     scratch += [dma((10,))] + [dma, dma((2, 3))] * 5 + [dma, dma((3,))]
     scratch += [pltpu.SemaphoreType.REGULAR((max(1, len(reaching(nz))), 2))]

time: 63.7 us -> 63.7 us (level)
  no operation moved by 1% of the time
where the time goes in v5:
time: 63.7 us; the launch traced here: 63.6 us
  Pallas kernels  62.9 us (99%)
  between operations  0.64 us (1%)
    pallas_call x1, Pallas kernels, shards(): pl.pallas_call(functools.partial(kernel, grid, nz), out_shape=(flat, duo,...  62 us

profile of v5, /device:TPU:1, one launch (start us, length us, event | category | flops | bytes accessed | tf_op | source)
XLA Modules:
  0.0 63.6 jit_solution(10867357551023131716)
XLA Ops:
  0.6 62.0 %shard_map.161 = (bf16[3,128,128]{2,1,0:T(8,128)(2,1)S(1)}, bf16[2,3,64,128]{3,2,1,0:T(8,128)(2,1)S(1)}, bf16[3,128,128]{2,1,0:T(8,128)(2,1)S(1)}, bf16[3,128,12...) custom-call(f32[3]{0:T(128)} %refs_0_.1, ...), custom_call_target="tpu_custom_call" | custom-call | tf_op jit(solution)/shard_map/pallas_call | solution.py:502
  62.6 0.9 %shard_map.162 = (bf16[3,128,128]{2,1,0:T(8,128)(2,1)}, bf16[2,3,64,128]{3,2,1,0:T(8,128)(2,1)}, bf16[3,128,128]{2,1,0:T(8,128)(2,1)}, bf16[3,128,128]{2,1,0:T(8...) custom-call(bf16[3,128,128]{2,1,0:T(8,128)(2,1)S(1)} %get-tuple-elem, ...), custom_call_target="tpu_custom_call" | custom-call | tf_op jit(solution)/shard_map/pallas_call | solution.py:510
